TPU v7x, 512 devices: a whole 4x8x8 slice. The times are simulated.
512 devices in a mesh: dp: 32 (over x, y), seq: 16 (over z, core).
Axes of the slice: x: 4, y: 8, z: 8, core: 2. Of those that a mesh axis runs over, the one named last changes fastest.
Arguments:
- residual_stream: bfloat16 [262144, 2048], P(('dp', 'seq')), parts along dimension 0, may hold values from -6 to 6
- octet_readout: bfloat16 [256, 2048], replicated, may hold values from -6 to 6
- downsampling_filter: bfloat16 [32, 256, 96], replicated, may hold values from -0.375 to 0.375
- sharpness_factor: float32 [8], replicated, may hold values from 4 to 20
- widening_filter: bfloat16 [32, 32, 256], replicated, may hold values from -2 to 2
Outputs:
- logits: bfloat16 [262144, 256], P(('dp', 'seq')), parts along dimension 0
There are 32 independent parts, one for each index of `dp`. A program takes and returns all parts, laid end to end along the dimension named above; an argument that names none is the same for every part. Nothing has to cross between parts.
All inputs are finite; a program needn't handle non-finite values.
Results may differ from a plain program's by a relative error of at most 0.0052.
Values may be sent and summed in bfloat16 or wider, within the bound.
A program may use at most 64 MiB of HBM per device.

v0:
```python
import jax
import jax.numpy as jnp
from jax import lax
from jax.sharding import PartitionSpec as P

SHORTEN = 4


def shifted_2(array, axis, by):
    count = lax.axis_size(axis)
    pairs = [(i, i + by) for i in range(count) if 0 <= i + by < count]
    return lax.ppermute(array, axis, pairs)


def passed_along(block, axis, distance):
    devices = range(lax.axis_size(axis))
    route = [((i - distance) % len(devices), i) for i in devices]
    return lax.ppermute(block, axis, route)


def normalize(vectors):
    return vectors * lax.rsqrt(jnp.sum(vectors * vectors, axis=-1, keepdims=True) + 1e-06)


def shorten(shifted, kernel_part, groups):
    byte_rows, model_width = shifted.shape
    windows = shifted.reshape(byte_rows // SHORTEN, SHORTEN, groups, model_width // groups)
    kernel = kernel_part.reshape(groups, SHORTEN, model_width // groups, kernel_part.shape[2])
    return jnp.einsum("jtgc,gtco->jgo", windows, kernel, preferred_element_type=jnp.float32)


def on_device(
    residual_stream, octet_readout, downsampling_filter, sharpness_factor, widening_filter
):
    byte_rows = residual_stream.shape[0]
    model_width = residual_stream.shape[1]
    groups = downsampling_filter.shape[0]
    group_width = model_width // groups
    per_group = downsampling_filter.shape[2] // 3
    attention_number = sharpness_factor.shape[0]
    head_size = groups * per_group // attention_number
    tokens_here = byte_rows // SHORTEN
    rim_rows = SHORTEN - 1
    left_rim = shifted_2(residual_stream[byte_rows - rim_rows :], "seq", 1)
    shifted = jnp.concatenate([left_rim, residual_stream[: byte_rows - rim_rows]], 0)
    mixed_out = shorten(shifted, downsampling_filter, groups)
    queries = normalize(
        mixed_out[:, :, :per_group].reshape(tokens_here, attention_number, head_size)
    ).astype(jnp.bfloat16)
    key_unit = normalize(
        mixed_out[:, :, per_group : 2 * per_group].reshape(tokens_here, attention_number, head_size)
    ).astype(jnp.bfloat16)
    values = (
        mixed_out[:, :, 2 * per_group :]
        .reshape(tokens_here, attention_number, head_size)
        .astype(jnp.bfloat16)
    )
    my_index = lax.axis_index("seq")
    seq_count = lax.axis_size("seq")
    first_token = my_index * tokens_here
    sharpness_vertical = sharpness_factor[:, None, None]
    query_pos = first_token + jnp.arange(tokens_here, dtype=jnp.int32)

    def attend(running, block_pair, offset):
        weighted, denom_sum = running
        block_keys, block_values = block_pair
        similarity_matrix = (
            jnp.einsum("jsg,isg->sji", queries, block_keys, preferred_element_type=jnp.float32)
            * sharpness_vertical
        )
        key_pos = offset + jnp.arange(block_keys.shape[0], dtype=jnp.int32)
        future_masked = jnp.logical_and(
            key_pos[None, :] <= query_pos[:, None], key_pos[None, :] >= 0
        )
        softmax_shares = jnp.where(
            future_masked[None],
            jnp.exp(similarity_matrix - sharpness_vertical),
            jnp.zeros((), jnp.float32),
        )
        denom_sum = denom_sum + jnp.sum(softmax_shares, axis=-1)
        weighted = weighted + jnp.einsum(
            "hqk,khd->qhd",
            softmax_shares.astype(jnp.bfloat16),
            block_values,
            preferred_element_type=jnp.float32,
        )
        return (weighted, denom_sum)

    initial_blank_state = (
        jnp.zeros((tokens_here, attention_number, head_size), jnp.float32),
        jnp.zeros((attention_number, tokens_here), jnp.float32),
    )

    def unchanged(running):
        return running

    running = attend(initial_blank_state, (key_unit, values), first_token)
    stacked = jnp.stack([key_unit, values], 0)

    def relay_step(step_index, state):
        moving, running = state
        moving = passed_along(moving, "seq", -1)
        source = (my_index + step_index) % seq_count

        def compute(running):
            return attend(running, (moving[0], moving[1]), source * tokens_here)

        running = lax.cond(source < my_index, compute, unchanged, running)
        return (moving, running)

    final_state = lax.fori_loop(1, seq_count, relay_step, (stacked, running))
    weighted, denom_sum = final_state[1]
    attended = (weighted / jnp.transpose(denom_sum)[:, :, None]).astype(jnp.bfloat16)
    attended = attended.reshape(tokens_here, groups, per_group)
    upsampled = jnp.einsum(
        "jgc,gcu->jgu", attended, widening_filter, preferred_element_type=jnp.float32
    )
    upsampled = (
        upsampled.reshape(tokens_here, groups, SHORTEN, group_width)
        .transpose(0, 2, 1, 3)
        .reshape(byte_rows, model_width)
    )
    hidden = residual_stream.astype(jnp.float32) + upsampled
    normed = (hidden * lax.rsqrt(jnp.mean(hidden * hidden, axis=-1, keepdims=True) + 1e-05)).astype(
        jnp.bfloat16
    )
    logits = lax.dot_general(
        normed, octet_readout, (((1,), (1,)), ((), ())), preferred_element_type=jnp.float32
    ) * model_width ** (-0.5)
    return logits.astype(jnp.bfloat16)


def solution(mesh):
    in_specs = (P(("dp", "seq"), None), P(), P(), P(), P())
    out_specs = P(("dp", "seq"), None)
    return jax.shard_map(
        on_device, mesh=mesh, in_specs=in_specs, out_specs=out_specs, check_vma=False
    )
```

profile of v0, /device:TPU:6, one launch (start us, length us, event | category | flops | bytes accessed | tf_op | source)
XLA Modules:
  0.0 237.4 jit_solution(6561855781226328031)
XLA Ops:
  0.0 0.9 slice.21
  0.9 1.9 collective-permute-start.1
  2.9 3.9 %copy.16 = bf16[32,256,96]{2,1,0:T(8,128)(2,1)} copy(bf16[32,256,96]{1,2,0:T(8,128)(2,1)} %param.11) | data formatting | bytes 3145728 | tf_op args[2]
  6.8 1.9 pad_maximum_fusion
  8.7 7.2 %reshape.176 = bf16[128,4,32,64]{3,2,1,0:T(8,128)(2,1)} reshape(bf16[512,2048]{1,0:T(8,128)(2,1)} %pad_maximum_fusion) | data formatting | bytes 4194304 | tf_op jit(solution)/shard_map/reshape | solution.py:27
  15.9 7.1 %fusion.15 = f32[128,32,96]{0,2,1:T(8,128)S(1)} fusion(bf16[32,4,64,96]{3,2,1,0:T(8,128)(2,1)S(1)} %bitcast.54, bf16[128,4,32,64]{3,2,1,0:T(8,128)(2,1)} %reshape.176), kind=kOutput, calls=%fused_computation.25 | convolution fusion | flops 201326592 | bytes 5242880 | tf_op jit(solution)/shard_map/jtgc,gtco->jgo/dot_general | solution.py:29
  24.0 1.0 copy.21
  25.4 1.4 fusion.26
  27.2 0.8 pad_maximum_fusion.1
  28.1 178.8 %while.20 = (s32[]{:T(128)}, bf16[2,128,8,128]{3,1,2,0:T(8,128)(2,1)}, f32[128,8,128]{2,0,1:T(8,128)S(1)}, f32[8,128]{1,0:T(8,128)S(1)}, s32[]{:T(128)}, /*index...) while((s32[]{:T(128)}, ...), condition=%wide.region_9.10_spmd.clone, body=%wide.region_5.0_spmd.clone.sunk | while | flops 67928592 | bytes 5558436 | solution.py:111
  28.1 8.0 %collective-permute-start = (bf16[2,128,8,128]{3,1,2,0:T(8,128)(2,1)}, bf16[2,128,8,128]{3,1,2,0:T(8,128)(2,1)S(1)}, u32[]{:S(2)}, u32[]{:S(2)}) collective-permute-start(bf16[2,128,8,128]{3,1,2,0:T(8,128)(2,1)} %get-tuple-element.384), channel_id=1, source_target_pairs={{1,0},{2,1},{3,2},{4,3},{5,4},{6,5},{7,6},{8,7},{9,8},{10,9},{11,1... | collective-permute-start | bytes 1572872 | tf_op jit(solution)/shard_map/while/body/eval_jaxpr/ppermute | solution.py:18
  36.1 7.0 %collective-permute-done = bf16[2,128,8,128]{3,1,2,0:T(8,128)(2,1)S(1)} collective-permute-done((bf16[2,128,8,128]{3,1,2,0:T(8,128)(2,1)}, bf16[2,128,8,128]{3,1,2,0:T(8,128)(2,1)S(1)}, u32[]{:S(2)}, u32[]{:S(2)}) %collective-permute-start) | collective-permute-done | bytes 524320 | tf_op jit(solution)/shard_map/while/body/eval_jaxpr/ppermute | solution.py:18
  43.9 3.8 %collective-permute-start = (bf16[2,128,8,128]{3,1,2,0:T(8,128)(2,1)}, bf16[2,128,8,128]{3,1,2,0:T(8,128)(2,1)S(1)}, u32[]{:S(2)}, u32[]{:S(2)}) collective-permute-start(bf16[2,128,8,128]{3,1,2,0:T(8,128)(2,1)} %get-tuple-element.384), channel_id=1, source_target_pairs={{1,0},{2,1},{3,2},{4,3},{5,4},{6,5},{7,6},{8,7},{9,8},{10,9},{11,1... | collective-permute-start | bytes 1572872 | tf_op jit(solution)/shard_map/while/body/eval_jaxpr/ppermute | solution.py:18
  47.8 7.0 %collective-permute-done = bf16[2,128,8,128]{3,1,2,0:T(8,128)(2,1)S(1)} collective-permute-done((bf16[2,128,8,128]{3,1,2,0:T(8,128)(2,1)}, bf16[2,128,8,128]{3,1,2,0:T(8,128)(2,1)S(1)}, u32[]{:S(2)}, u32[]{:S(2)}) %collective-permute-start) | collective-permute-done | bytes 524320 | tf_op jit(solution)/shard_map/while/body/eval_jaxpr/ppermute | solution.py:18
  55.6 3.8 %collective-permute-start = (bf16[2,128,8,128]{3,1,2,0:T(8,128)(2,1)}, bf16[2,128,8,128]{3,1,2,0:T(8,128)(2,1)S(1)}, u32[]{:S(2)}, u32[]{:S(2)}) collective-permute-start(bf16[2,128,8,128]{3,1,2,0:T(8,128)(2,1)} %get-tuple-element.384), channel_id=1, source_target_pairs={{1,0},{2,1},{3,2},{4,3},{5,4},{6,5},{7,6},{8,7},{9,8},{10,9},{11,1... | collective-permute-start | bytes 1572872 | tf_op jit(solution)/shard_map/while/body/eval_jaxpr/ppermute | solution.py:18
  59.4 7.0 %collective-permute-done = bf16[2,128,8,128]{3,1,2,0:T(8,128)(2,1)S(1)} collective-permute-done((bf16[2,128,8,128]{3,1,2,0:T(8,128)(2,1)}, bf16[2,128,8,128]{3,1,2,0:T(8,128)(2,1)S(1)}, u32[]{:S(2)}, u32[]{:S(2)}) %collective-permute-start) | collective-permute-done | bytes 524320 | tf_op jit(solution)/shard_map/while/body/eval_jaxpr/ppermute | solution.py:18
  67.2 3.8 %collective-permute-start = (bf16[2,128,8,128]{3,1,2,0:T(8,128)(2,1)}, bf16[2,128,8,128]{3,1,2,0:T(8,128)(2,1)S(1)}, u32[]{:S(2)}, u32[]{:S(2)}) collective-permute-start(bf16[2,128,8,128]{3,1,2,0:T(8,128)(2,1)} %get-tuple-element.384), channel_id=1, source_target_pairs={{1,0},{2,1},{3,2},{4,3},{5,4},{6,5},{7,6},{8,7},{9,8},{10,9},{11,1... | collective-permute-start | bytes 1572872 | tf_op jit(solution)/shard_map/while/body/eval_jaxpr/ppermute | solution.py:18
  71.0 7.0 %collective-permute-done = bf16[2,128,8,128]{3,1,2,0:T(8,128)(2,1)S(1)} collective-permute-done((bf16[2,128,8,128]{3,1,2,0:T(8,128)(2,1)}, bf16[2,128,8,128]{3,1,2,0:T(8,128)(2,1)S(1)}, u32[]{:S(2)}, u32[]{:S(2)}) %collective-permute-start) | collective-permute-done | bytes 524320 | tf_op jit(solution)/shard_map/while/body/eval_jaxpr/ppermute | solution.py:18
  78.8 3.8 %collective-permute-start = (bf16[2,128,8,128]{3,1,2,0:T(8,128)(2,1)}, bf16[2,128,8,128]{3,1,2,0:T(8,128)(2,1)S(1)}, u32[]{:S(2)}, u32[]{:S(2)}) collective-permute-start(bf16[2,128,8,128]{3,1,2,0:T(8,128)(2,1)} %get-tuple-element.384), channel_id=1, source_target_pairs={{1,0},{2,1},{3,2},{4,3},{5,4},{6,5},{7,6},{8,7},{9,8},{10,9},{11,1... | collective-permute-start | bytes 1572872 | tf_op jit(solution)/shard_map/while/body/eval_jaxpr/ppermute | solution.py:18
  82.7 7.0 %collective-permute-done = bf16[2,128,8,128]{3,1,2,0:T(8,128)(2,1)S(1)} collective-permute-done((bf16[2,128,8,128]{3,1,2,0:T(8,128)(2,1)}, bf16[2,128,8,128]{3,1,2,0:T(8,128)(2,1)S(1)}, u32[]{:S(2)}, u32[]{:S(2)}) %collective-permute-start) | collective-permute-done | bytes 524320 | tf_op jit(solution)/shard_map/while/body/eval_jaxpr/ppermute | solution.py:18
  89.7 0.8 copy.47
  90.5 3.8 %collective-permute-start = (bf16[2,128,8,128]{3,1,2,0:T(8,128)(2,1)}, bf16[2,128,8,128]{3,1,2,0:T(8,128)(2,1)S(1)}, u32[]{:S(2)}, u32[]{:S(2)}) collective-permute-start(bf16[2,128,8,128]{3,1,2,0:T(8,128)(2,1)} %get-tuple-element.384), channel_id=1, source_target_pairs={{1,0},{2,1},{3,2},{4,3},{5,4},{6,5},{7,6},{8,7},{9,8},{10,9},{11,1... | collective-permute-start | bytes 1572872 | tf_op jit(solution)/shard_map/while/body/eval_jaxpr/ppermute | solution.py:18
  94.3 7.0 %collective-permute-done = bf16[2,128,8,128]{3,1,2,0:T(8,128)(2,1)S(1)} collective-permute-done((bf16[2,128,8,128]{3,1,2,0:T(8,128)(2,1)}, bf16[2,128,8,128]{3,1,2,0:T(8,128)(2,1)S(1)}, u32[]{:S(2)}, u32[]{:S(2)}) %collective-permute-start) | collective-permute-done | bytes 524320 | tf_op jit(solution)/shard_map/while/body/eval_jaxpr/ppermute | solution.py:18
  101.3 0.8 copy.47
  102.1 3.8 %collective-permute-start = (bf16[2,128,8,128]{3,1,2,0:T(8,128)(2,1)}, bf16[2,128,8,128]{3,1,2,0:T(8,128)(2,1)S(1)}, u32[]{:S(2)}, u32[]{:S(2)}) collective-permute-start(bf16[2,128,8,128]{3,1,2,0:T(8,128)(2,1)} %get-tuple-element.384), channel_id=1, source_target_pairs={{1,0},{2,1},{3,2},{4,3},{5,4},{6,5},{7,6},{8,7},{9,8},{10,9},{11,1... | collective-permute-start | bytes 1572872 | tf_op jit(solution)/shard_map/while/body/eval_jaxpr/ppermute | solution.py:18
  106.0 7.0 %collective-permute-done = bf16[2,128,8,128]{3,1,2,0:T(8,128)(2,1)S(1)} collective-permute-done((bf16[2,128,8,128]{3,1,2,0:T(8,128)(2,1)}, bf16[2,128,8,128]{3,1,2,0:T(8,128)(2,1)S(1)}, u32[]{:S(2)}, u32[]{:S(2)}) %collective-permute-start) | collective-permute-done | bytes 524320 | tf_op jit(solution)/shard_map/while/body/eval_jaxpr/ppermute | solution.py:18
  113.8 3.8 %collective-permute-start = (bf16[2,128,8,128]{3,1,2,0:T(8,128)(2,1)}, bf16[2,128,8,128]{3,1,2,0:T(8,128)(2,1)S(1)}, u32[]{:S(2)}, u32[]{:S(2)}) collective-permute-start(bf16[2,128,8,128]{3,1,2,0:T(8,128)(2,1)} %get-tuple-element.384), channel_id=1, source_target_pairs={{1,0},{2,1},{3,2},{4,3},{5,4},{6,5},{7,6},{8,7},{9,8},{10,9},{11,1... | collective-permute-start | bytes 1572872 | tf_op jit(solution)/shard_map/while/body/eval_jaxpr/ppermute | solution.py:18
  117.6 7.0 %collective-permute-done = bf16[2,128,8,128]{3,1,2,0:T(8,128)(2,1)S(1)} collective-permute-done((bf16[2,128,8,128]{3,1,2,0:T(8,128)(2,1)}, bf16[2,128,8,128]{3,1,2,0:T(8,128)(2,1)S(1)}, u32[]{:S(2)}, u32[]{:S(2)}) %collective-permute-start) | collective-permute-done | bytes 524320 | tf_op jit(solution)/shard_map/while/body/eval_jaxpr/ppermute | solution.py:18
  125.4 3.8 %collective-permute-start = (bf16[2,128,8,128]{3,1,2,0:T(8,128)(2,1)}, bf16[2,128,8,128]{3,1,2,0:T(8,128)(2,1)S(1)}, u32[]{:S(2)}, u32[]{:S(2)}) collective-permute-start(bf16[2,128,8,128]{3,1,2,0:T(8,128)(2,1)} %get-tuple-element.384), channel_id=1, source_target_pairs={{1,0},{2,1},{3,2},{4,3},{5,4},{6,5},{7,6},{8,7},{9,8},{10,9},{11,1... | collective-permute-start | bytes 1572872 | tf_op jit(solution)/shard_map/while/body/eval_jaxpr/ppermute | solution.py:18
  129.2 7.0 %collective-permute-done = bf16[2,128,8,128]{3,1,2,0:T(8,128)(2,1)S(1)} collective-permute-done((bf16[2,128,8,128]{3,1,2,0:T(8,128)(2,1)}, bf16[2,128,8,128]{3,1,2,0:T(8,128)(2,1)S(1)}, u32[]{:S(2)}, u32[]{:S(2)}) %collective-permute-start) | collective-permute-done | bytes 524320 | tf_op jit(solution)/shard_map/while/body/eval_jaxpr/ppermute | solution.py:18
  137.0 3.8 %collective-permute-start = (bf16[2,128,8,128]{3,1,2,0:T(8,128)(2,1)}, bf16[2,128,8,128]{3,1,2,0:T(8,128)(2,1)S(1)}, u32[]{:S(2)}, u32[]{:S(2)}) collective-permute-start(bf16[2,128,8,128]{3,1,2,0:T(8,128)(2,1)} %get-tuple-element.384), channel_id=1, source_target_pairs={{1,0},{2,1},{3,2},{4,3},{5,4},{6,5},{7,6},{8,7},{9,8},{10,9},{11,1... | collective-permute-start | bytes 1572872 | tf_op jit(solution)/shard_map/while/body/eval_jaxpr/ppermute | solution.py:18
  140.9 7.0 %collective-permute-done = bf16[2,128,8,128]{3,1,2,0:T(8,128)(2,1)S(1)} collective-permute-done((bf16[2,128,8,128]{3,1,2,0:T(8,128)(2,1)}, bf16[2,128,8,128]{3,1,2,0:T(8,128)(2,1)S(1)}, u32[]{:S(2)}, u32[]{:S(2)}) %collective-permute-start) | collective-permute-done | bytes 524320 | tf_op jit(solution)/shard_map/while/body/eval_jaxpr/ppermute | solution.py:18
  148.7 3.8 %collective-permute-start = (bf16[2,128,8,128]{3,1,2,0:T(8,128)(2,1)}, bf16[2,128,8,128]{3,1,2,0:T(8,128)(2,1)S(1)}, u32[]{:S(2)}, u32[]{:S(2)}) collective-permute-start(bf16[2,128,8,128]{3,1,2,0:T(8,128)(2,1)} %get-tuple-element.384), channel_id=1, source_target_pairs={{1,0},{2,1},{3,2},{4,3},{5,4},{6,5},{7,6},{8,7},{9,8},{10,9},{11,1... | collective-permute-start | bytes 1572872 | tf_op jit(solution)/shard_map/while/body/eval_jaxpr/ppermute | solution.py:18
  152.5 7.0 %collective-permute-done = bf16[2,128,8,128]{3,1,2,0:T(8,128)(2,1)S(1)} collective-permute-done((bf16[2,128,8,128]{3,1,2,0:T(8,128)(2,1)}, bf16[2,128,8,128]{3,1,2,0:T(8,128)(2,1)S(1)}, u32[]{:S(2)}, u32[]{:S(2)}) %collective-permute-start) | collective-permute-done | bytes 524320 | tf_op jit(solution)/shard_map/while/body/eval_jaxpr/ppermute | solution.py:18
  160.3 3.8 %collective-permute-start = (bf16[2,128,8,128]{3,1,2,0:T(8,128)(2,1)}, bf16[2,128,8,128]{3,1,2,0:T(8,128)(2,1)S(1)}, u32[]{:S(2)}, u32[]{:S(2)}) collective-permute-start(bf16[2,128,8,128]{3,1,2,0:T(8,128)(2,1)} %get-tuple-element.384), channel_id=1, source_target_pairs={{1,0},{2,1},{3,2},{4,3},{5,4},{6,5},{7,6},{8,7},{9,8},{10,9},{11,1... | collective-permute-start | bytes 1572872 | tf_op jit(solution)/shard_map/while/body/eval_jaxpr/ppermute | solution.py:18
  164.2 7.0 %collective-permute-done = bf16[2,128,8,128]{3,1,2,0:T(8,128)(2,1)S(1)} collective-permute-done((bf16[2,128,8,128]{3,1,2,0:T(8,128)(2,1)}, bf16[2,128,8,128]{3,1,2,0:T(8,128)(2,1)S(1)}, u32[]{:S(2)}, u32[]{:S(2)}) %collective-permute-start) | collective-permute-done | bytes 524320 | tf_op jit(solution)/shard_map/while/body/eval_jaxpr/ppermute | solution.py:18
  172.0 3.8 %collective-permute-start = (bf16[2,128,8,128]{3,1,2,0:T(8,128)(2,1)}, bf16[2,128,8,128]{3,1,2,0:T(8,128)(2,1)S(1)}, u32[]{:S(2)}, u32[]{:S(2)}) collective-permute-start(bf16[2,128,8,128]{3,1,2,0:T(8,128)(2,1)} %get-tuple-element.384), channel_id=1, source_target_pairs={{1,0},{2,1},{3,2},{4,3},{5,4},{6,5},{7,6},{8,7},{9,8},{10,9},{11,1... | collective-permute-start | bytes 1572872 | tf_op jit(solution)/shard_map/while/body/eval_jaxpr/ppermute | solution.py:18
  175.8 7.0 %collective-permute-done = bf16[2,128,8,128]{3,1,2,0:T(8,128)(2,1)S(1)} collective-permute-done((bf16[2,128,8,128]{3,1,2,0:T(8,128)(2,1)}, bf16[2,128,8,128]{3,1,2,0:T(8,128)(2,1)S(1)}, u32[]{:S(2)}, u32[]{:S(2)}) %collective-permute-start) | collective-permute-done | bytes 524320 | tf_op jit(solution)/shard_map/while/body/eval_jaxpr/ppermute | solution.py:18
  183.6 3.8 %collective-permute-start = (bf16[2,128,8,128]{3,1,2,0:T(8,128)(2,1)}, bf16[2,128,8,128]{3,1,2,0:T(8,128)(2,1)S(1)}, u32[]{:S(2)}, u32[]{:S(2)}) collective-permute-start(bf16[2,128,8,128]{3,1,2,0:T(8,128)(2,1)} %get-tuple-element.384), channel_id=1, source_target_pairs={{1,0},{2,1},{3,2},{4,3},{5,4},{6,5},{7,6},{8,7},{9,8},{10,9},{11,1... | collective-permute-start | bytes 1572872 | tf_op jit(solution)/shard_map/while/body/eval_jaxpr/ppermute | solution.py:18
  187.4 7.0 %collective-permute-done = bf16[2,128,8,128]{3,1,2,0:T(8,128)(2,1)S(1)} collective-permute-done((bf16[2,128,8,128]{3,1,2,0:T(8,128)(2,1)}, bf16[2,128,8,128]{3,1,2,0:T(8,128)(2,1)S(1)}, u32[]{:S(2)}, u32[]{:S(2)}) %collective-permute-start) | collective-permute-done | bytes 524320 | tf_op jit(solution)/shard_map/while/body/eval_jaxpr/ppermute | solution.py:18
  195.2 3.8 %collective-permute-start = (bf16[2,128,8,128]{3,1,2,0:T(8,128)(2,1)}, bf16[2,128,8,128]{3,1,2,0:T(8,128)(2,1)S(1)}, u32[]{:S(2)}, u32[]{:S(2)}) collective-permute-start(bf16[2,128,8,128]{3,1,2,0:T(8,128)(2,1)} %get-tuple-element.384), channel_id=1, source_target_pairs={{1,0},{2,1},{3,2},{4,3},{5,4},{6,5},{7,6},{8,7},{9,8},{10,9},{11,1... | collective-permute-start | bytes 1572872 | tf_op jit(solution)/shard_map/while/body/eval_jaxpr/ppermute | solution.py:18
  199.1 7.0 %collective-permute-done = bf16[2,128,8,128]{3,1,2,0:T(8,128)(2,1)S(1)} collective-permute-done((bf16[2,128,8,128]{3,1,2,0:T(8,128)(2,1)}, bf16[2,128,8,128]{3,1,2,0:T(8,128)(2,1)S(1)}, u32[]{:S(2)}, u32[]{:S(2)}) %collective-permute-start) | collective-permute-done | bytes 524320 | tf_op jit(solution)/shard_map/while/body/eval_jaxpr/ppermute | solution.py:18
  207.2 2.7 %convolution_bitcast_fusion.1 = f32[128,32,256]{2,0,1:T(8,128)} fusion(bf16[128,32,32]{0,2,1:T(8,128)(2,1)S(1)} %bitcast.56, bf16[32,32,256]{2,1,0:T(8,128)(2,1)S(1)} %copy-done.5), kind=kOutput, calls=%fused_computation.21 | convolution fusion | flops 67108864 | bytes 4980736 | tf_op jit(solution)/shard_map/jgc,gcu->jgu/dot_general | solution.py:115
  209.8 5.6 %copy.25 = f32[128,32,256]{0,2,1:T(8,128)} copy(f32[128,32,256]{2,0,1:T(8,128)} %convolution_bitcast_fusion.1) | data formatting | bytes 8388608 | tf_op jit(solution)/shard_map/jgc,gcu->jgu/transpose | solution.py:115
  215.4 9.1 %copy.26 = f32[128,4,32,64]{3,2,1,0:T(8,128)} copy(f32[128,4,32,64]{0,3,1,2:T(8,128)} %bitcast.49) | data formatting | bytes 8388608 | tf_op jit(solution)/shard_map/transpose | solution.py:120
  224.5 8.0 %reshape.183 = f32[512,2048]{1,0:T(8,128)} reshape(f32[128,4,32,64]{3,2,1,0:T(8,128)} %copy.26) | data formatting | bytes 8388608 | tf_op jit(solution)/shard_map/reshape | solution.py:121
  232.5 3.0 %multiply_reduce_fusion = f32[512]{0:T(512)S(1)} fusion(f32[512,2048]{1,0:T(8,128)} %reshape.183, bf16[512,2048]{1,0:T(8,128)(2,1)S(1)} %copy-done.3), kind=kLoop, calls=%fused_computation.19 | loop fusion | flops 4193792 | bytes 6293504 | tf_op jit(solution)/shard_map/reduce_sum | solution.py:124
  236.0 1.5 fusion.22
  (77 shorter events, 12.9 us)
Async XLA Ops:
  0.0 235.5 %copy-start = (bf16[256,2048]{1,0:T(8,128)(2,1)S(1)}, bf16[256,2048]{1,0:T(8,128)(2,1)}, u32[]{:S(2)}) copy-start(bf16[256,2048]{1,0:T(8,128)(2,1)} %param.10) | copy-start | bytes 3145732
  0.0 6.8 %copy-start.2 = (bf16[512,2048]{1,0:T(8,128)(2,1)S(1)}, bf16[512,2048]{1,0:T(8,128)(2,1)}, u32[]{:S(2)}) copy-start(bf16[512,2048]{1,0:T(8,128)(2,1)} %param.9) | copy-start | bytes 6291460
  0.9 5.9 %collective-permute-start.1 = (bf16[3,2048]{1,0:T(4,128)(2,1)S(1)}, bf16[3,2048]{1,0:T(4,128)(2,1)S(1)}, u32[]{:S(2)}, u32[]{:S(2)}) collective-permute-start(bf16[3,2048]{1,0:T(4,128)(2,1)S(1)} %slice.21), channel_id=1, source_target_pairs={{0,1},{1,2},{2,3},{3,4},{4,5},{5,6},{6,7},{7,8},{8,9},{9,10},{10,1... | collective-permute-start | bytes 36872 | tf_op jit(solution)/shard_map/ppermute | solution.py:12
  8.7 7.2 %copy-start.4 = (bf16[32,256,96]{2,1,0:T(8,128)(2,1)S(1)}, bf16[32,256,96]{2,1,0:T(8,128)(2,1)}, u32[]{:S(2)}) copy-start(bf16[32,256,96]{2,1,0:T(8,128)(2,1)} %copy.16) | copy-start | bytes 4718596
  23.0 2.4 %copy-start.6 = (f32[8]{0:T(128)S(1)}, f32[8]{0:T(128)}, u32[]{:S(2)}) copy-start(f32[8]{0:T(128)} %param.12) | copy-start | bytes 100
  28.1 179.1 %copy-start.5 = (bf16[32,32,256]{2,1,0:T(8,128)(2,1)S(1)}, bf16[32,32,256]{2,1,0:T(8,128)(2,1)}, u32[]{:S(2)}) copy-start(bf16[32,32,256]{2,1,0:T(8,128)(2,1)} %param.13) | copy-start | bytes 1572868
  28.1 15.0 %collective-permute-start = (bf16[2,128,8,128]{3,1,2,0:T(8,128)(2,1)}, bf16[2,128,8,128]{3,1,2,0:T(8,128)(2,1)S(1)}, u32[]{:S(2)}, u32[]{:S(2)}) collective-permute-start(bf16[2,128,8,128]{3,1,2,0:T(8,128)(2,1)} %get-tuple-element.384), channel_id=1, source_target_pairs={{1,0},{2,1},{3,2},{4,3},{5,4},{6,5},{7,6},{8,7},{9,8},{10,9},{11,1... | collective-permute-start | bytes 1572872 | tf_op jit(solution)/shard_map/while/body/eval_jaxpr/ppermute | solution.py:18
  43.9 10.8 %collective-permute-start = (bf16[2,128,8,128]{3,1,2,0:T(8,128)(2,1)}, bf16[2,128,8,128]{3,1,2,0:T(8,128)(2,1)S(1)}, u32[]{:S(2)}, u32[]{:S(2)}) collective-permute-start(bf16[2,128,8,128]{3,1,2,0:T(8,128)(2,1)} %get-tuple-element.384), channel_id=1, source_target_pairs={{1,0},{2,1},{3,2},{4,3},{5,4},{6,5},{7,6},{8,7},{9,8},{10,9},{11,1... | collective-permute-start | bytes 1572872 | tf_op jit(solution)/shard_map/while/body/eval_jaxpr/ppermute | solution.py:18
  55.6 10.8 %collective-permute-start = (bf16[2,128,8,128]{3,1,2,0:T(8,128)(2,1)}, bf16[2,128,8,128]{3,1,2,0:T(8,128)(2,1)S(1)}, u32[]{:S(2)}, u32[]{:S(2)}) collective-permute-start(bf16[2,128,8,128]{3,1,2,0:T(8,128)(2,1)} %get-tuple-element.384), channel_id=1, source_target_pairs={{1,0},{2,1},{3,2},{4,3},{5,4},{6,5},{7,6},{8,7},{9,8},{10,9},{11,1... | collective-permute-start | bytes 1572872 | tf_op jit(solution)/shard_map/while/body/eval_jaxpr/ppermute | solution.py:18
  67.2 10.8 %collective-permute-start = (bf16[2,128,8,128]{3,1,2,0:T(8,128)(2,1)}, bf16[2,128,8,128]{3,1,2,0:T(8,128)(2,1)S(1)}, u32[]{:S(2)}, u32[]{:S(2)}) collective-permute-start(bf16[2,128,8,128]{3,1,2,0:T(8,128)(2,1)} %get-tuple-element.384), channel_id=1, source_target_pairs={{1,0},{2,1},{3,2},{4,3},{5,4},{6,5},{7,6},{8,7},{9,8},{10,9},{11,1... | collective-permute-start | bytes 1572872 | tf_op jit(solution)/shard_map/while/body/eval_jaxpr/ppermute | solution.py:18
  78.8 10.8 %collective-permute-start = (bf16[2,128,8,128]{3,1,2,0:T(8,128)(2,1)}, bf16[2,128,8,128]{3,1,2,0:T(8,128)(2,1)S(1)}, u32[]{:S(2)}, u32[]{:S(2)}) collective-permute-start(bf16[2,128,8,128]{3,1,2,0:T(8,128)(2,1)} %get-tuple-element.384), channel_id=1, source_target_pairs={{1,0},{2,1},{3,2},{4,3},{5,4},{6,5},{7,6},{8,7},{9,8},{10,9},{11,1... | collective-permute-start | bytes 1572872 | tf_op jit(solution)/shard_map/while/body/eval_jaxpr/ppermute | solution.py:18
  90.5 10.8 %collective-permute-start = (bf16[2,128,8,128]{3,1,2,0:T(8,128)(2,1)}, bf16[2,128,8,128]{3,1,2,0:T(8,128)(2,1)S(1)}, u32[]{:S(2)}, u32[]{:S(2)}) collective-permute-start(bf16[2,128,8,128]{3,1,2,0:T(8,128)(2,1)} %get-tuple-element.384), channel_id=1, source_target_pairs={{1,0},{2,1},{3,2},{4,3},{5,4},{6,5},{7,6},{8,7},{9,8},{10,9},{11,1... | collective-permute-start | bytes 1572872 | tf_op jit(solution)/shard_map/while/body/eval_jaxpr/ppermute | solution.py:18
  102.1 10.8 %collective-permute-start = (bf16[2,128,8,128]{3,1,2,0:T(8,128)(2,1)}, bf16[2,128,8,128]{3,1,2,0:T(8,128)(2,1)S(1)}, u32[]{:S(2)}, u32[]{:S(2)}) collective-permute-start(bf16[2,128,8,128]{3,1,2,0:T(8,128)(2,1)} %get-tuple-element.384), channel_id=1, source_target_pairs={{1,0},{2,1},{3,2},{4,3},{5,4},{6,5},{7,6},{8,7},{9,8},{10,9},{11,1... | collective-permute-start | bytes 1572872 | tf_op jit(solution)/shard_map/while/body/eval_jaxpr/ppermute | solution.py:18
  113.8 10.8 %collective-permute-start = (bf16[2,128,8,128]{3,1,2,0:T(8,128)(2,1)}, bf16[2,128,8,128]{3,1,2,0:T(8,128)(2,1)S(1)}, u32[]{:S(2)}, u32[]{:S(2)}) collective-permute-start(bf16[2,128,8,128]{3,1,2,0:T(8,128)(2,1)} %get-tuple-element.384), channel_id=1, source_target_pairs={{1,0},{2,1},{3,2},{4,3},{5,4},{6,5},{7,6},{8,7},{9,8},{10,9},{11,1... | collective-permute-start | bytes 1572872 | tf_op jit(solution)/shard_map/while/body/eval_jaxpr/ppermute | solution.py:18
  125.4 10.8 %collective-permute-start = (bf16[2,128,8,128]{3,1,2,0:T(8,128)(2,1)}, bf16[2,128,8,128]{3,1,2,0:T(8,128)(2,1)S(1)}, u32[]{:S(2)}, u32[]{:S(2)}) collective-permute-start(bf16[2,128,8,128]{3,1,2,0:T(8,128)(2,1)} %get-tuple-element.384), channel_id=1, source_target_pairs={{1,0},{2,1},{3,2},{4,3},{5,4},{6,5},{7,6},{8,7},{9,8},{10,9},{11,1... | collective-permute-start | bytes 1572872 | tf_op jit(solution)/shard_map/while/body/eval_jaxpr/ppermute | solution.py:18
  137.0 10.8 %collective-permute-start = (bf16[2,128,8,128]{3,1,2,0:T(8,128)(2,1)}, bf16[2,128,8,128]{3,1,2,0:T(8,128)(2,1)S(1)}, u32[]{:S(2)}, u32[]{:S(2)}) collective-permute-start(bf16[2,128,8,128]{3,1,2,0:T(8,128)(2,1)} %get-tuple-element.384), channel_id=1, source_target_pairs={{1,0},{2,1},{3,2},{4,3},{5,4},{6,5},{7,6},{8,7},{9,8},{10,9},{11,1... | collective-permute-start | bytes 1572872 | tf_op jit(solution)/shard_map/while/body/eval_jaxpr/ppermute | solution.py:18
  148.7 10.8 %collective-permute-start = (bf16[2,128,8,128]{3,1,2,0:T(8,128)(2,1)}, bf16[2,128,8,128]{3,1,2,0:T(8,128)(2,1)S(1)}, u32[]{:S(2)}, u32[]{:S(2)}) collective-permute-start(bf16[2,128,8,128]{3,1,2,0:T(8,128)(2,1)} %get-tuple-element.384), channel_id=1, source_target_pairs={{1,0},{2,1},{3,2},{4,3},{5,4},{6,5},{7,6},{8,7},{9,8},{10,9},{11,1... | collective-permute-start | bytes 1572872 | tf_op jit(solution)/shard_map/while/body/eval_jaxpr/ppermute | solution.py:18
  160.3 10.8 %collective-permute-start = (bf16[2,128,8,128]{3,1,2,0:T(8,128)(2,1)}, bf16[2,128,8,128]{3,1,2,0:T(8,128)(2,1)S(1)}, u32[]{:S(2)}, u32[]{:S(2)}) collective-permute-start(bf16[2,128,8,128]{3,1,2,0:T(8,128)(2,1)} %get-tuple-element.384), channel_id=1, source_target_pairs={{1,0},{2,1},{3,2},{4,3},{5,4},{6,5},{7,6},{8,7},{9,8},{10,9},{11,1... | collective-permute-start | bytes 1572872 | tf_op jit(solution)/shard_map/while/body/eval_jaxpr/ppermute | solution.py:18
  172.0 10.8 %collective-permute-start = (bf16[2,128,8,128]{3,1,2,0:T(8,128)(2,1)}, bf16[2,128,8,128]{3,1,2,0:T(8,128)(2,1)S(1)}, u32[]{:S(2)}, u32[]{:S(2)}) collective-permute-start(bf16[2,128,8,128]{3,1,2,0:T(8,128)(2,1)} %get-tuple-element.384), channel_id=1, source_target_pairs={{1,0},{2,1},{3,2},{4,3},{5,4},{6,5},{7,6},{8,7},{9,8},{10,9},{11,1... | collective-permute-start | bytes 1572872 | tf_op jit(solution)/shard_map/while/body/eval_jaxpr/ppermute | solution.py:18
  183.6 10.8 %collective-permute-start = (bf16[2,128,8,128]{3,1,2,0:T(8,128)(2,1)}, bf16[2,128,8,128]{3,1,2,0:T(8,128)(2,1)S(1)}, u32[]{:S(2)}, u32[]{:S(2)}) collective-permute-start(bf16[2,128,8,128]{3,1,2,0:T(8,128)(2,1)} %get-tuple-element.384), channel_id=1, source_target_pairs={{1,0},{2,1},{3,2},{4,3},{5,4},{6,5},{7,6},{8,7},{9,8},{10,9},{11,1... | collective-permute-start | bytes 1572872 | tf_op jit(solution)/shard_map/while/body/eval_jaxpr/ppermute | solution.py:18
  195.2 10.8 %collective-permute-start = (bf16[2,128,8,128]{3,1,2,0:T(8,128)(2,1)}, bf16[2,128,8,128]{3,1,2,0:T(8,128)(2,1)S(1)}, u32[]{:S(2)}, u32[]{:S(2)}) collective-permute-start(bf16[2,128,8,128]{3,1,2,0:T(8,128)(2,1)} %get-tuple-element.384), channel_id=1, source_target_pairs={{1,0},{2,1},{3,2},{4,3},{5,4},{6,5},{7,6},{8,7},{9,8},{10,9},{11,1... | collective-permute-start | bytes 1572872 | tf_op jit(solution)/shard_map/while/body/eval_jaxpr/ppermute | solution.py:18
  224.5 8.0 %copy-start.3 = (bf16[512,2048]{1,0:T(8,128)(2,1)S(1)}, bf16[512,2048]{1,0:T(8,128)(2,1)}, u32[]{:S(2)}) copy-start(bf16[512,2048]{1,0:T(8,128)(2,1)} %param.9) | copy-start | bytes 6291460
  232.5 3.4 %copy-start.1 = (f32[512,2048]{1,0:T(8,128)S(1)}, f32[512,2048]{1,0:T(8,128)}, u32[]{:S(2)}) copy-start(f32[512,2048]{1,0:T(8,128)} %reshape.183) | copy-start | bytes 12582916
where the time goes:
time: 238 us; the launch traced here: 237 us
  waiting for transfers between devices  105 us (44%)
  starting transfers between devices  63.5 us (27%)
  local copies, waits for them, and re-layouts  49 us (21%)
  matrix products  12.8 us (5%)
  other arithmetic  6.54 us (3%)
    ppermute x15, waiting for transfers between devices, passed_along(): return lax.ppermute(block, axis, route)  105 us
    ppermute x15, starting transfers between devices, passed_along(): return lax.ppermute(block, axis, route)  61.7 us
    while x15, local copies, waits for them, and re-layouts  11.8 us
    transpose x1, local copies, waits for them, and re-layouts, on_device(): upsampled = upsampled.reshape(tokens_here, groups, SHORTEN, group_width)....  9.14 us
    reshape x1, local copies, waits for them, and re-layouts, on_device(): upsampled = upsampled.reshape(tokens_here, groups, SHORTEN, group_width)....  7.98 us
    reshape x1, local copies, waits for them, and re-layouts, shorten(): shifted.reshape(byte_rows // SHORTEN, SHORTEN, groups, model_width // gro...  7.23 us
    dot_general x1, matrix products, shorten(): jnp.einsum('jtgc,gtco->jgo', windows, kernel, preferred_element_type=jnp....  7.09 us
    transpose x1, local copies, waits for them, and re-layouts, on_device(): jnp.einsum('jgc,gcu->jgu', attended, widening_filter, preferred_element_t...  5.56 us
  transfers between devices with their start and end apart: 16, of which 15 were waited for; matrix products, arithmetic and copies ran while one was open for 2% of the time, Pallas kernels for 0%

commit v1 on v0

--- a/solution.py
+++ b/solution.py
@@ -56,60 +56,31 @@
         .astype(jnp.bfloat16)
     )
     my_index = lax.axis_index("seq")
-    seq_count = lax.axis_size("seq")
     first_token = my_index * tokens_here
     sharpness_vertical = sharpness_factor[:, None, None]
     query_pos = first_token + jnp.arange(tokens_here, dtype=jnp.int32)
 
-    def attend(running, block_pair, offset):
-        weighted, denom_sum = running
-        block_keys, block_values = block_pair
-        similarity_matrix = (
-            jnp.einsum("jsg,isg->sji", queries, block_keys, preferred_element_type=jnp.float32)
-            * sharpness_vertical
-        )
-        key_pos = offset + jnp.arange(block_keys.shape[0], dtype=jnp.int32)
-        future_masked = jnp.logical_and(
-            key_pos[None, :] <= query_pos[:, None], key_pos[None, :] >= 0
-        )
-        softmax_shares = jnp.where(
-            future_masked[None],
-            jnp.exp(similarity_matrix - sharpness_vertical),
-            jnp.zeros((), jnp.float32),
-        )
-        denom_sum = denom_sum + jnp.sum(softmax_shares, axis=-1)
-        weighted = weighted + jnp.einsum(
-            "hqk,khd->qhd",
-            softmax_shares.astype(jnp.bfloat16),
-            block_values,
-            preferred_element_type=jnp.float32,
-        )
-        return (weighted, denom_sum)
-
-    initial_blank_state = (
-        jnp.zeros((tokens_here, attention_number, head_size), jnp.float32),
-        jnp.zeros((attention_number, tokens_here), jnp.float32),
+    stacked = jnp.stack([key_unit, values], 0)
+    gathered = lax.all_gather(stacked, "seq", axis=1, tiled=True)
+    all_keys, all_values = gathered[0], gathered[1]
+    similarity_matrix = (
+        jnp.einsum("jsg,isg->sji", queries, all_keys, preferred_element_type=jnp.float32)
+        * sharpness_vertical
     )
-
-    def unchanged(running):
-        return running
-
-    running = attend(initial_blank_state, (key_unit, values), first_token)
-    stacked = jnp.stack([key_unit, values], 0)
-
-    def relay_step(step_index, state):
-        moving, running = state
-        moving = passed_along(moving, "seq", -1)
-        source = (my_index + step_index) % seq_count
-
-        def compute(running):
-            return attend(running, (moving[0], moving[1]), source * tokens_here)
-
-        running = lax.cond(source < my_index, compute, unchanged, running)
-        return (moving, running)
-
-    final_state = lax.fori_loop(1, seq_count, relay_step, (stacked, running))
-    weighted, denom_sum = final_state[1]
+    key_pos = jnp.arange(all_keys.shape[0], dtype=jnp.int32)
+    future_masked = key_pos[None, :] <= query_pos[:, None]
+    softmax_shares = jnp.where(
+        future_masked[None],
+        jnp.exp(similarity_matrix - sharpness_vertical),
+        jnp.zeros((), jnp.float32),
+    )
+    denom_sum = jnp.sum(softmax_shares, axis=-1)
+    weighted = jnp.einsum(
+        "hqk,khd->qhd",
+        softmax_shares.astype(jnp.bfloat16),
+        all_values,
+        preferred_element_type=jnp.float32,
+    )
     attended = (weighted / jnp.transpose(denom_sum)[:, :, None]).astype(jnp.bfloat16)
     attended = attended.reshape(tokens_here, groups, per_group)
     upsampled = jnp.einsum(

time: 238 us -> 156 us (0.66)
  starting transfers between devices: 63.5 us -> 1.87 us
  waiting for transfers between devices: 105 us -> 63.1 us
  matrix products: 12.8 us -> 26.1 us
  between operations: 0.2 us -> 13.5 us
  local copies, waits for them, and re-layouts: 49 us -> 39.9 us
  other arithmetic: 6.54 us -> 9.4 us
    ppermute x15 -> x0, waiting for transfers between devices: 105 us -> none  [passed_along(): return lax.ppermute(block, axis, route)]
    all_gather x0 -> x1, waiting for transfers between devices: none -> 63.1 us  [on_device(): gathered = lax.all_gather(stacked, 'seq', axis=1, tiled=True)]
    ppermute x15 -> x0, starting transfers between devices: 61.7 us -> none  [passed_along(): return lax.ppermute(block, axis, route)]
    dot_general x2, matrix products: 1.6 us -> 14.1 us  [the longest x1 8.29 us: on_device(): jnp.einsum('jsg,isg->sji', queries, all_keys, preferred_element_type=jnp....]
    while x16 -> x0, local copies, waits for them, and re-layouts: 12 us -> none
  transfers between devices with their start and end apart: 16 -> 2, of which waited for: 15 -> 1; matrix products, arithmetic and copies ran while one was open for 2% -> 4% of each run, Pallas kernels for 0% -> 0%
where the time goes in v1:
time: 156 us; the launch traced here: 154 us
  waiting for transfers between devices  63.1 us (40%)
  local copies, waits for them, and re-layouts  39.9 us (26%)
  matrix products  26.1 us (17%)
  between operations  13.5 us (9%)
  other arithmetic  9.4 us (6%)
  starting transfers between devices  1.87 us (1%)
    all_gather x1, waiting for transfers between devices, on_device(): gathered = lax.all_gather(stacked, 'seq', axis=1, tiled=True)  63.1 us
    transpose x1, local copies, waits for them, and re-layouts, on_device(): upsampled = upsampled.reshape(tokens_here, groups, SHORTEN, group_width)....  9.14 us
    dot_general x1, matrix products, on_device(): jnp.einsum('jsg,isg->sji', queries, all_keys, preferred_element_type=jnp....  8.29 us
    reshape x1, local copies, waits for them, and re-layouts, on_device(): upsampled = upsampled.reshape(tokens_here, groups, SHORTEN, group_width)....  7.82 us
    dot_general x1, matrix products, shorten(): jnp.einsum('jtgc,gtco->jgo', windows, kernel, preferred_element_type=jnp....  7.76 us
    reshape x1, local copies, waits for them, and re-layouts, shorten(): shifted.reshape(byte_rows // SHORTEN, SHORTEN, groups, model_width // gro...  7.08 us
    dot_general x1, matrix products, on_device(): jnp.einsum('hqk,khd->qhd', softmax_shares.astype(jnp.bfloat16), all_value...  5.85 us
    transpose x1, local copies, waits for them, and re-layouts, on_device(): jnp.einsum('jgc,gcu->jgu', attended, widening_filter, preferred_element_t...  5.56 us
  transfers between devices with their start and end apart: 2, of which 1 were waited for; matrix products, arithmetic and copies ran while one was open for 4% of the time, Pallas kernels for 0%

profile of v1, /device:TPU:6, one launch (start us, length us, event | category | flops | bytes accessed | tf_op | source)
XLA Modules:
  0.0 153.8 jit_solution(6165816291397608881)
XLA Ops:
  6.5 0.0 copy-start
  6.5 0.0 copy-start.2
  6.5 0.0 all-gather.2.cloned.1.call-start
  6.5 0.9 slice.22
  7.5 1.9 %collective-permute-start = (bf16[3,2048]{1,0:T(4,128)(2,1)S(1)}, bf16[3,2048]{1,0:T(4,128)(2,1)S(1)}, u32[]{:S(2)}, u32[]{:S(2)}) collective-permute-start(bf16[3,2048]{1,0:T(4,128)(2,1)S(1)} %slice.22), channel_id=1, source_target_pairs={{0,1},{1,2},{2,3},{3,4},{4,5},{5,6},{6,7},{7,8},{8,9},{9,10},{10,1... | collective-permute-start | bytes 36872 | tf_op jit(solution)/shard_map/ppermute | solution.py:12
  9.3 3.9 %copy.12 = bf16[32,256,96]{2,1,0:T(8,128)(2,1)} copy(bf16[32,256,96]{1,2,0:T(8,128)(2,1)} %param.7) | data formatting | bytes 3145728 | tf_op args[2]
  13.2 0.0 collective-permute-done
  13.2 0.0 copy-done.2
  13.2 1.9 %pad_maximum_fusion = bf16[512,2048]{1,0:T(8,128)(2,1)} fusion(bf16[509,2048]{1,0:T(8,128)(2,1)S(1)} %bitcast.45, bf16[3,2048]{1,0:T(4,128)(2,1)S(1)} %collective-permute-done), kind=kLoop, calls=%fused_computation.17 | loop fusion | flops 4194304 | bytes 4194304 | tf_op jit(solution)/shard_map/concatenate | solution.py:45
  15.2 7.1 %reshape.93 = bf16[128,4,32,64]{3,2,1,0:T(8,128)(2,1)} reshape(bf16[512,2048]{1,0:T(8,128)(2,1)} %pad_maximum_fusion) | data formatting | bytes 4194304 | tf_op jit(solution)/shard_map/reshape | solution.py:27
  22.2 7.8 %fusion.12 = f32[128,32,96]{0,2,1:T(8,128)S(1)} fusion(bf16[32,4,64,96]{3,2,1,0:T(8,128)(2,1)} %bitcast.47, bf16[128,4,32,64]{3,2,1,0:T(8,128)(2,1)} %reshape.93), kind=kOutput, calls=%fused_computation.19 | convolution fusion | flops 201326592 | bytes 5242880 | tf_op jit(solution)/shard_map/jtgc,gtco->jgo/dot_general | solution.py:29
  30.0 0.0 copy-start.5
  30.1 1.1 multiply_reduce_fusion.1
  31.2 0.9 copy.15
  32.1 2.1 %copy.14 = f32[1,128,8,128]{3,1,2,0:T(8,128)} copy(f32[1,128,8,128]{1,3,2,0:T(8,128)} %bitcast.49) | data formatting | bytes 1048576 | tf_op jit(solution)/shard_map/reshape | solution.py:51
  34.1 1.2 multiply_convert_fusion.7
  35.4 1.9 %pad_maximum_fusion.1 = bf16[2,128,8,128]{3,1,2,0:T(8,128)(2,1)} fusion(bf16[1,128,8,128]{3,1,2,0:T(8,128)(2,1)} %copy.15, bf16[1,128,8,128]{3,1,2,0:T(8,128)(2,1)S(1)} %multiply_convert_fusion.7), kind=kLoop, calls=%fused_computation.27 | loop fusion | flops 262144 | bytes 1048576 | tf_op jit(solution)/shard_map/stack | solution.py:63
  37.2 0.0 all-gather.2.cloned.1.call-update
  37.3 0.2 iota_compare_fusion
  37.5 2.0 %copy.16 = f32[128,8,128]{2,0,1:T(8,128)} copy(f32[128,8,128]{0,2,1:T(8,128)} %bitcast.48) | data formatting | bytes 1048576 | tf_op jit(solution)/shard_map/reshape | solution.py:48
  39.6 63.1 %all-gather.2.cloned.1.call-done = bf16[2,2048,8,128]{3,1,2,0:T(8,128)(2,1)} async-done(((bf16[2,128,8,128]{3,1,2,0:T(8,128)(2,1)}), bf16[2,2048,8,128]{3,1,2,0:T(8,128)(2,1)}) %all-gather.2.cloned.1.call-update) | async-done | bytes 8388624 | tf_op jit(solution)/shard_map/all_gather | solution.py:64
  102.7 0.0 copy-done.5
  102.7 0.0 copy-start.4
  102.7 8.3 %fusion = (f32[8,128]{1,0:T(8,128)S(1)}, f32[8,128,2048]{2,1,0:T(8,128)}) fusion(f32[8]{0:T(128)S(1)} %copy-done.5, pred[128,2048]{1,0:T(8,128)(4,1)S(1)} %iota_compare_fusion, bf16[2,2048,8,128]{3,1,2,0:T(8,128)(2,1)} %all-gather.2.cloned.1.call-done, f32[128,8,128]{2,0,1:T(8,128)} %copy.16, f32[128,8]{0,1:T(8,128)S(1)} %add_rsqrt_fusion), kind=kOutput, calls=%fused_computation.1 | convolution fusion | flops 545520640 | bytes 13377568 | tf_op jit(solution)/shard_map/jsg,isg->sji/dot_general | solution.py:67
  111.0 0.0 copy-done.4
  111.0 0.0 copy-start.3
  111.0 5.8 %fusion.23 = bf16[128,8,128]{0,2,1:T(8,128)(2,1)S(1)} fusion(f32[8,128,2048]{2,1,0:T(8,128)} %get-tuple-element.10, f32[8]{0:T(128)S(1)} %copy-done.5, pred[128,2048]{1,0:T(8,128)(4,1)S(1)} %iota_compare_fusion, bf16[2,2048,8,128]{3,1,2,0:T(8,128)(2,1)S(1)} %copy-done.4, f32[128,8]{0,1:T(8,128)S(1)} %bitcast.54), kind=kOutput, calls=%fused_computation.25 | convolution fusion | flops 545521664 | bytes 13111808 | tf_op jit(solution)/shard_map/hqk,khd->qhd/dot_general | solution.py:78
  116.8 0.0 copy-done.3
  116.8 2.7 %convolution_bitcast_fusion = f32[128,32,256]{2,0,1:T(8,128)} fusion(bf16[128,32,32]{0,2,1:T(8,128)(2,1)S(1)} %bitcast.51, bf16[32,32,256]{2,1,0:T(8,128)(2,1)S(1)} %copy-done.3), kind=kOutput, calls=%fused_computation.15 | convolution fusion | flops 67108864 | bytes 4980736 | tf_op jit(solution)/shard_map/jgc,gcu->jgu/dot_general | solution.py:86
  119.5 5.6 %copy.18 = f32[128,32,256]{0,2,1:T(8,128)} copy(f32[128,32,256]{2,0,1:T(8,128)} %convolution_bitcast_fusion) | data formatting | bytes 8388608 | tf_op jit(solution)/shard_map/jgc,gcu->jgu/transpose | solution.py:86
  125.1 9.1 %copy.19 = f32[128,4,32,64]{3,2,1,0:T(8,128)} copy(f32[128,4,32,64]{0,3,1,2:T(8,128)} %bitcast.46) | data formatting | bytes 8388608 | tf_op jit(solution)/shard_map/transpose | solution.py:91
  134.2 7.8 %reshape.99 = f32[512,2048]{1,0:T(8,128)} reshape(f32[128,4,32,64]{3,2,1,0:T(8,128)} %copy.19) | data formatting | bytes 8388608 | tf_op jit(solution)/shard_map/reshape | solution.py:92
  142.1 0.0 copy-start.1
  142.1 3.0 %multiply_reduce_fusion = f32[512]{0:T(512)S(1)} fusion(f32[512,2048]{1,0:T(8,128)} %reshape.99, bf16[512,2048]{1,0:T(8,128)(2,1)S(1)} %copy-done.2), kind=kLoop, calls=%fused_computation.10 | loop fusion | flops 4193792 | bytes 6293504 | tf_op jit(solution)/shard_map/reduce_sum | solution.py:95
  145.0 0.0 copy-done
  145.0 0.5 copy-done.1
  145.5 1.5 fusion.19
  (7 shorter events, 0.1 us)
Async XLA Ops:
  6.5 138.5 %copy-start = (bf16[256,2048]{1,0:T(8,128)(2,1)S(1)}, bf16[256,2048]{1,0:T(8,128)(2,1)}, u32[]{:S(2)}) copy-start(bf16[256,2048]{1,0:T(8,128)(2,1)} %param.6) | copy-start | bytes 3145732
  6.5 6.7 %copy-start.2 = (bf16[512,2048]{1,0:T(8,128)(2,1)S(1)}, bf16[512,2048]{1,0:T(8,128)(2,1)}, u32[]{:S(2)}) copy-start(bf16[512,2048]{1,0:T(8,128)(2,1)} %param.5) | copy-start | bytes 6291460
  6.5 96.1 %all-gather.2.cloned.1.call-start = ((), (), s32[]{:S(2)}) async-start(), calls=%async_computation | async-start | bytes 8912896 | tf_op jit(solution)/shard_map/all_gather | solution.py:64
  7.5 5.7 %collective-permute-start = (bf16[3,2048]{1,0:T(4,128)(2,1)S(1)}, bf16[3,2048]{1,0:T(4,128)(2,1)S(1)}, u32[]{:S(2)}, u32[]{:S(2)}) collective-permute-start(bf16[3,2048]{1,0:T(4,128)(2,1)S(1)} %slice.22), channel_id=1, source_target_pairs={{0,1},{1,2},{2,3},{3,4},{4,5},{5,6},{6,7},{7,8},{8,9},{9,10},{10,1... | collective-permute-start | bytes 36872 | tf_op jit(solution)/shard_map/ppermute | solution.py:12
  30.0 72.7 %copy-start.5 = (f32[8]{0:T(128)S(1)}, f32[8]{0:T(128)}, u32[]{:S(2)}) copy-start(f32[8]{0:T(128)} %param.8) | copy-start | bytes 100
  102.7 8.3 %copy-start.4 = (bf16[2,2048,8,128]{3,1,2,0:T(8,128)(2,1)S(1)}, bf16[2,2048,8,128]{3,1,2,0:T(8,128)(2,1)}, u32[]{:S(2)}) copy-start(bf16[2,2048,8,128]{3,1,2,0:T(8,128)(2,1)} %all-gather.2.cloned.1.call-done) | copy-start | bytes 25165828
  111.0 5.9 %copy-start.3 = (bf16[32,32,256]{2,1,0:T(8,128)(2,1)S(1)}, bf16[32,32,256]{2,1,0:T(8,128)(2,1)}, u32[]{:S(2)}) copy-start(bf16[32,32,256]{2,1,0:T(8,128)(2,1)} %param.9) | copy-start | bytes 1572868
  142.1 3.4 %copy-start.1 = (f32[512,2048]{1,0:T(8,128)S(1)}, f32[512,2048]{1,0:T(8,128)}, u32[]{:S(2)}) copy-start(f32[512,2048]{1,0:T(8,128)} %reshape.99) | copy-start | bytes 12582916
Sparse Core Ops, SparseCore 0:
  37.4 65.2 all-gather.1

commit v2 on v1

v2 whole, which is shorter than its diff:
```python
import jax
import jax.numpy as jnp
from jax import lax
from jax.experimental import pallas as pl
from jax.experimental.pallas import tpu as pltpu
from jax.sharding import PartitionSpec as P

SHORTEN = 4


def shifted_2(array, axis, by):
    count = lax.axis_size(axis)
    pairs = [(i, i + by) for i in range(count) if 0 <= i + by < count]
    return lax.ppermute(array, axis, pairs)


def normalize(vectors):
    return vectors * lax.rsqrt(jnp.sum(vectors * vectors, axis=-1, keepdims=True) + 1e-06)


def shorten(shifted, kernel_part, groups):
    byte_rows, model_width = shifted.shape
    windows = shifted.reshape(byte_rows // SHORTEN, SHORTEN, groups, model_width // groups)
    kernel = kernel_part.reshape(groups, SHORTEN, model_width // groups, kernel_part.shape[2])
    return jnp.einsum("jtgc,gtco->jgo", windows, kernel, preferred_element_type=jnp.float32)


def widening_blocks(widening_filter, heads):
    groups, per_group, span = widening_filter.shape
    gph = groups // heads
    width = span // SHORTEN
    wf = widening_filter.reshape(heads, gph, per_group, SHORTEN, width)
    wf = wf.transpose(3, 0, 1, 2, 4)[:, :, :, :, None, :]
    eye = jnp.eye(gph, dtype=jnp.bool_)[:, None, :, None]
    blocks = jnp.where(eye, wf, jnp.zeros((), wf.dtype))
    return blocks.reshape(SHORTEN, heads, gph * per_group, gph * width)


def post_kernel(idx_ref, sharp_ref, q_ref, kv_ref, wup_ref, res_ref, oct_ref, out_ref, att_scr):
    me = idx_ref[0]
    heads, tq, hd = q_ref.shape
    f32, bf16 = jnp.float32, jnp.bfloat16
    qpos = me * tq + lax.broadcasted_iota(jnp.int32, (tq, tq), 0)
    kio = lax.broadcasted_iota(jnp.int32, (tq, tq), 1)
    for h in range(heads):
        q = q_ref[h]
        sharp = sharp_ref[h]

        def body(d, carry, q=q, sharp=sharp, h=h):
            num, den = carry
            s = lax.dot_general(
                q, kv_ref[0, d, h], (((1,), (1,)), ((), ())), preferred_element_type=f32
            ) * sharp
            w = jnp.where(d * tq + kio <= qpos, jnp.exp(s - sharp), jnp.zeros((), f32))
            den = den + jnp.sum(w, axis=1, keepdims=True)
            num = num + jnp.dot(w.astype(bf16), kv_ref[1, d, h], preferred_element_type=f32)
            return num, den

        num, den = lax.fori_loop(
            0, me + 1, body, (jnp.zeros((tq, hd), f32), jnp.zeros((tq, 1), f32))
        )
        att_scr[:, h * hd : (h + 1) * hd] = (num / den).astype(bf16)

    rows, width = res_ref.shape
    row_blocks = rows // 128
    tok_blk = 128 // SHORTEN
    n_chunks = wup_ref.shape[1]
    cin = wup_ref.shape[2]
    cout = wup_ref.shape[3]
    r_i = lax.broadcasted_iota(jnp.int32, (128, tok_blk), 0)
    j_i = lax.broadcasted_iota(jnp.int32, (128, tok_blk), 1)
    for rb in range(row_blocks):
        a_blk = att_scr[pl.ds(rb * tok_blk, tok_blk), :]
        expanded = []
        for t in range(SHORTEN):
            sel = (r_i == SHORTEN * j_i + t).astype(bf16)
            expanded.append(jnp.dot(sel, a_blk, preferred_element_type=f32).astype(bf16))
        hid = []
        ss = jnp.zeros((128, 1), f32)
        for k in range(n_chunks):
            u = jnp.dot(expanded[0][:, k * cin : (k + 1) * cin], wup_ref[0, k], preferred_element_type=f32)
            for t in range(1, SHORTEN):
                u = u + jnp.dot(
                    expanded[t][:, k * cin : (k + 1) * cin], wup_ref[t, k], preferred_element_type=f32
                )
            hcol = res_ref[pl.ds(rb * 128, 128), pl.ds(k * cout, cout)].astype(f32) + u
            hid.append(hcol)
            ss = ss + jnp.sum(hcol * hcol, axis=1, keepdims=True)
        scale = lax.rsqrt(ss / width + 1e-05)
        acc = None
        for k in range(n_chunks):
            part = lax.dot_general(
                (hid[k] * scale).astype(bf16),
                oct_ref[:, pl.ds(k * cout, cout)],
                (((1,), (1,)), ((), ())),
                preferred_element_type=f32,
            )
            acc = part if acc is None else acc + part
        out_ref[pl.ds(rb * 128, 128), :] = (acc * width ** (-0.5)).astype(out_ref.dtype)


def on_device(
    residual_stream, octet_readout, downsampling_filter, sharpness_factor, widening_filter
):
    byte_rows = residual_stream.shape[0]
    model_width = residual_stream.shape[1]
    groups = downsampling_filter.shape[0]
    per_group = downsampling_filter.shape[2] // 3
    attention_number = sharpness_factor.shape[0]
    head_size = groups * per_group // attention_number
    tokens_here = byte_rows // SHORTEN
    rim_rows = SHORTEN - 1
    left_rim = shifted_2(residual_stream[byte_rows - rim_rows :], "seq", 1)
    shifted = jnp.concatenate([left_rim, residual_stream[: byte_rows - rim_rows]], 0)
    mixed_out = shorten(shifted, downsampling_filter, groups)

    def heads_first(x):
        return x.reshape(tokens_here, attention_number, head_size).transpose(1, 0, 2)

    queries = heads_first(normalize(
        mixed_out[:, :, :per_group].reshape(tokens_here, attention_number, head_size)
    ).astype(jnp.bfloat16))
    key_unit = heads_first(normalize(
        mixed_out[:, :, per_group : 2 * per_group].reshape(tokens_here, attention_number, head_size)
    ).astype(jnp.bfloat16))
    values = heads_first(mixed_out[:, :, 2 * per_group :].astype(jnp.bfloat16))
    stacked = jnp.stack([key_unit, values], 0)[:, None]
    gathered = lax.all_gather(stacked, "seq", axis=1, tiled=True)
    my_index = lax.axis_index("seq").astype(jnp.int32).reshape(1)
    wup = widening_blocks(widening_filter, attention_number)
    vmem = pl.BlockSpec(memory_space=pltpu.VMEM)
    smem = pl.BlockSpec(memory_space=pltpu.SMEM)
    return pl.pallas_call(
        post_kernel,
        out_shape=jax.ShapeDtypeStruct((byte_rows, octet_readout.shape[0]), jnp.bfloat16),
        in_specs=[smem, smem, vmem, vmem, vmem, vmem, vmem],
        out_specs=vmem,
        scratch_shapes=[pltpu.VMEM((tokens_here, attention_number * head_size), jnp.bfloat16)],
        compiler_params=pltpu.CompilerParams(vmem_limit_bytes=60 * 1024 * 1024),
    )(my_index, sharpness_factor, queries, gathered, wup, residual_stream, octet_readout)


def solution(mesh):
    in_specs = (P(("dp", "seq"), None), P(), P(), P(), P())
    out_specs = P(("dp", "seq"), None)
    return jax.shard_map(
        on_device, mesh=mesh, in_specs=in_specs, out_specs=out_specs, check_vma=False
    )
```

time: 156 us -> 145 us (0.929)
  the two profiles are of different devices: /device:TPU:6 before, /device:TPU:449 now
where the time goes in v2:
time: 145 us
  Pallas kernels  48.8 us (34%)
  waiting for transfers between devices  44.6 us (31%)
  local copies, waits for them, and re-layouts  23.9 us (16%)
  between operations  13.5 us (9%)
  matrix products  7.08 us (5%)
  other arithmetic  5.72 us (4%)
    pallas_call x1, Pallas kernels, on_device(): pl.pallas_call(post_kernel, out_shape=jax.ShapeDtypeStruct((byte_rows, oc...  48.8 us
    all_gather x1, waiting for transfers between devices, on_device(): gathered = lax.all_gather(stacked, 'seq', axis=1, tiled=True)  44.5 us
    broadcast_in_dim x4, local copies, waits for them, and re-layouts, widening_blocks(): blocks = jnp.where(eye, wf, jnp.zeros((), wf.dtype))  10.6 us
    reshape x1, local copies, waits for them, and re-layouts, shorten(): shifted.reshape(byte_rows // SHORTEN, SHORTEN, groups, model_width // gro...  7.23 us
    dot_general x1, matrix products, shorten(): jnp.einsum('jtgc,gtco->jgo', windows, kernel, preferred_element_type=jnp....  7.08 us
    unnamed x7, local copies, waits for them, and re-layouts  3.88 us
  transfers between devices with their start and end apart: 2, of which 1 were waited for; matrix products, arithmetic and copies ran while one was open for 12% of the time, Pallas kernels for 0%

profile of v2, /device:TPU:449, one launch (start us, length us, event | category | flops | bytes accessed | tf_op | source)
XLA Modules:
  0.0 144.9 jit_solution(14985749418896589955)
XLA Ops:
  6.5 0.0 copy-start
  6.5 0.0 all-gather.3.cloned.1.call-start
  6.5 0.9 slice.16
  7.5 1.3 collective-permute-start
  8.8 3.9 %copy.10 = bf16[32,256,96]{2,1,0:T(8,128)(2,1)} copy(bf16[32,256,96]{1,2,0:T(8,128)(2,1)} %param.7) | data formatting | bytes 3145728 | tf_op args[2]
  12.6 0.0 collective-permute-done
  12.6 0.0 copy-done
  12.6 1.9 %pad_maximum_fusion = bf16[512,2048]{1,0:T(8,128)(2,1)} fusion(bf16[509,2048]{1,0:T(8,128)(2,1)S(1)} %bitcast.25, bf16[3,2048]{1,0:T(4,128)(2,1)S(1)} %collective-permute-done), kind=kLoop, calls=%fused_computation.2 | loop fusion | flops 4194304 | bytes 4194304 | tf_op jit(solution)/shard_map/concatenate | solution.py:114
  14.5 0.0 copy-start.1
  14.5 7.2 %reshape.40 = bf16[128,4,32,64]{3,2,1,0:T(8,128)(2,1)} reshape(bf16[512,2048]{1,0:T(8,128)(2,1)} %pad_maximum_fusion) | data formatting | bytes 4194304 | tf_op jit(solution)/shard_map/reshape | solution.py:23
  21.7 0.0 copy-done.1
  21.7 7.1 %fusion.2 = f32[128,32,96]{0,2,1:T(8,128)S(1)} fusion(bf16[32,4,64,96]{3,2,1,0:T(8,128)(2,1)S(1)} %bitcast.28, bf16[128,4,32,64]{3,2,1,0:T(8,128)(2,1)} %reshape.40), kind=kOutput, calls=%fused_computation.4 | convolution fusion | flops 201326592 | bytes 5242880 | tf_op jit(solution)/shard_map/jtgc,gtco->jgo/dot_general | solution.py:25
  28.8 0.3 multiply_reduce_fusion
  29.2 0.0 copy-start.2
  29.2 0.2 copy.13
  29.4 0.2 copy.14
  29.6 0.2 fusion.6
  29.8 0.9 pad_maximum_fusion.1
  30.7 0.0 all-gather.3.cloned.1.call-update
  30.7 0.0 copy-done.2
  30.7 0.4 reshape.45
  31.1 0.2 copy.15
  31.4 4.4 %broadcast_in_dim.37 = bf16[4,8,4,32,4,64]{5,4,3,2,1,0:T(4,128)(2,1)} broadcast(bf16[4,8,4,32,64]{4,3,2,1,0:T(8,128)(2,1)S(1)} %copy.15), dimensions={0,1,2,3,5} | broadcast | bytes 2621440 | tf_op jit(solution)/shard_map/jit(_where)/broadcast_in_dim | solution.py:35
  35.8 6.0 %broadcast_in_dim.38 = bf16[4,8,128,256]{3,2,1,0:T(8,128)(2,1)S(1)} reshape(bf16[4,8,4,32,4,64]{5,4,3,2,1,0:T(4,128)(2,1)} %broadcast_in_dim.37) | data formatting | bytes 4194304 | tf_op jit(solution)/shard_map/jit(_where)/broadcast_in_dim | solution.py:35
  41.8 0.1 broadcast_in_dim.34
  41.9 0.2 broadcast_in_dim.35
  42.0 1.5 %broadcast_select_fusion.wup_ref = bf16[4,8,128,256]{3,2,1,0:T(8,128)(2,1)} fusion(bf16[4,8,128,256]{3,2,1,0:T(8,128)(2,1)S(1)} %broadcast_in_dim.38, pred[128,256]{1,0:T(8,128)(4,1)S(1)} %broadcast_in_dim.35), kind=kLoop, calls=%fused_computation.3 | loop fusion | flops 1048576 | bytes 4227072 | tf_op jit(solution)/shard_map/jit(_where)/select_n | solution.py:35
  43.6 0.2 copy.12
  43.8 0.9 fusion.5.q_ref
  44.7 44.5 %all-gather.3.cloned.1.call-done = bf16[2,128,128,128]{3,2,1,0:T(8,128)(2,1)} async-done(((bf16[2,8,128,128]{3,2,1,0:T(8,128)(2,1)}), bf16[2,128,128,128]{3,2,1,0:T(8,128)(2,1)}) %all-gather.3.cloned.1.call-update) | async-done | bytes 8388624 | tf_op jit(solution)/shard_map/all_gather | solution.py:128
  89.3 48.8 %shard_map.55 = bf16[512,256]{1,0:T(8,128)(2,1)} custom-call(s32[1]{0:T(128)} %bitcast.idx_ref, f32[8]{0:T(128)} %sharp_ref.1, bf16[8,128,128]{2,1,0:T(8,128)(2,1)} %fusion.5.q_ref, bf16[2,16,8,128,128]{4,3,2,1,0:T(8,128)(2,1)} %bitcast.26, bf16[4,8,128,256]{3,2,1,0:T(8,128)(2,1)} %broadcast_select_fusion.wup_ref, bf16[512,2048]{1,0:T(8,128)(2,1)} %res_ref.1, ...), custom_call_target="tpu_custom_call" | custom-call | tf_op jit(solution)/shard_map/pallas_call | solution.py:133
  (6 shorter events, 0.1 us)
Async XLA Ops:
  6.5 6.1 %copy-start = (bf16[512,2048]{1,0:T(8,128)(2,1)S(1)}, bf16[512,2048]{1,0:T(8,128)(2,1)}, u32[]{:S(2)}) copy-start(bf16[512,2048]{1,0:T(8,128)(2,1)} %res_ref.1) | copy-start | bytes 6291460
  6.5 82.7 %all-gather.3.cloned.1.call-start = ((), (), s32[]{:S(2)}) async-start(), calls=%async_computation | async-start | bytes 8912896 | tf_op jit(solution)/shard_map/all_gather | solution.py:128
  7.5 5.2 %collective-permute-start = (bf16[3,2048]{1,0:T(4,128)(2,1)S(1)}, bf16[3,2048]{1,0:T(4,128)(2,1)S(1)}, u32[]{:S(2)}, u32[]{:S(2)}) collective-permute-start(bf16[3,2048]{1,0:T(4,128)(2,1)S(1)} %slice.16), channel_id=1, source_target_pairs={{0,1},{1,2},{2,3},{3,4},{4,5},{5,6},{6,7},{7,8},{8,9},{9,10},{10,1... | collective-permute-start | bytes 36872 | tf_op jit(solution)/shard_map/ppermute | solution.py:14
  14.5 7.2 %copy-start.1 = (bf16[32,256,96]{2,1,0:T(8,128)(2,1)S(1)}, bf16[32,256,96]{2,1,0:T(8,128)(2,1)}, u32[]{:S(2)}) copy-start(bf16[32,256,96]{2,1,0:T(8,128)(2,1)} %copy.10) | copy-start | bytes 4718596
  29.2 1.5 %copy-start.2 = (bf16[32,32,256]{2,1,0:T(8,128)(2,1)S(1)}, bf16[32,32,256]{2,1,0:T(8,128)(2,1)}, u32[]{:S(2)}) copy-start(bf16[32,32,256]{2,1,0:T(8,128)(2,1)} %param.9) | copy-start | bytes 1572868
Sparse Core Ops, SparseCore 0:
  30.8 58.4 all-gather.2

commit v3 on v2

--- a/solution.py
+++ b/solution.py
@@ -18,13 +18,6 @@
     return vectors * lax.rsqrt(jnp.sum(vectors * vectors, axis=-1, keepdims=True) + 1e-06)
 
 
-def shorten(shifted, kernel_part, groups):
-    byte_rows, model_width = shifted.shape
-    windows = shifted.reshape(byte_rows // SHORTEN, SHORTEN, groups, model_width // groups)
-    kernel = kernel_part.reshape(groups, SHORTEN, model_width // groups, kernel_part.shape[2])
-    return jnp.einsum("jtgc,gtco->jgo", windows, kernel, preferred_element_type=jnp.float32)
-
-
 def widening_blocks(widening_filter, heads):
     groups, per_group, span = widening_filter.shape
     gph = groups // heads
@@ -34,6 +27,48 @@
     eye = jnp.eye(gph, dtype=jnp.bool_)[:, None, :, None]
     blocks = jnp.where(eye, wf, jnp.zeros((), wf.dtype))
     return blocks.reshape(SHORTEN, heads, gph * per_group, gph * width)
+
+
+def shortening_blocks(downsampling_filter, heads):
+    groups, span, outs = downsampling_filter.shape
+    gph = groups // heads
+    width = span // SHORTEN
+    per_group = outs // 3
+    w = downsampling_filter.reshape(heads, gph, SHORTEN, width, 3, per_group)
+    w = w.transpose(2, 0, 1, 3, 4, 5)[:, :, :, :, :, None, :]
+    eye = jnp.eye(gph, dtype=jnp.bool_)[:, None, None, :, None]
+    blocks = jnp.where(eye, w, jnp.zeros((), w.dtype))
+    return blocks.reshape(SHORTEN, heads, gph * width, 3 * gph * per_group)
+
+
+def shorten_kernel(res_ref, rim_ref, wd_ref, q_ref, kv_ref):
+    f32, bf16 = jnp.float32, jnp.bfloat16
+    rows = res_ref.shape[0]
+    tokens = rows // SHORTEN
+    heads = wd_ref.shape[1]
+    cin = wd_ref.shape[2]
+    hd = wd_ref.shape[3] // 3
+    j_i = lax.broadcasted_iota(jnp.int32, (tokens, rows), 0)
+    r_i = lax.broadcasted_iota(jnp.int32, (tokens, rows), 1)
+    first = lax.broadcasted_iota(jnp.int32, (tokens, 1), 0) == 0
+    res = res_ref[...]
+    picked = []
+    for t in range(SHORTEN):
+        sel = (r_i == SHORTEN * j_i + t - (SHORTEN - 1)).astype(bf16)
+        x = jnp.dot(sel, res, preferred_element_type=f32).astype(bf16)
+        if t < SHORTEN - 1:
+            x = jnp.where(first, rim_ref[pl.ds(t, 1), :], x)
+        picked.append(x)
+    for k in range(heads):
+        acc = None
+        for t in range(SHORTEN):
+            part = jnp.dot(picked[t][:, k * cin : (k + 1) * cin], wd_ref[t, k], preferred_element_type=f32)
+            acc = part if acc is None else acc + part
+        q = acc[:, :hd]
+        key = acc[:, hd : 2 * hd]
+        q_ref[k] = normalize(q).astype(bf16)
+        kv_ref[0, 0, k] = normalize(key).astype(bf16)
+        kv_ref[1, 0, k] = acc[:, 2 * hd :].astype(bf16)
 
 
 def post_kernel(idx_ref, sharp_ref, q_ref, kv_ref, wup_ref, res_ref, oct_ref, out_ref, att_scr):
@@ -103,7 +138,6 @@
     residual_stream, octet_readout, downsampling_filter, sharpness_factor, widening_filter
 ):
     byte_rows = residual_stream.shape[0]
-    model_width = residual_stream.shape[1]
     groups = downsampling_filter.shape[0]
     per_group = downsampling_filter.shape[2] // 3
     attention_number = sharpness_factor.shape[0]
@@ -111,25 +145,22 @@
     tokens_here = byte_rows // SHORTEN
     rim_rows = SHORTEN - 1
     left_rim = shifted_2(residual_stream[byte_rows - rim_rows :], "seq", 1)
-    shifted = jnp.concatenate([left_rim, residual_stream[: byte_rows - rim_rows]], 0)
-    mixed_out = shorten(shifted, downsampling_filter, groups)
-
-    def heads_first(x):
-        return x.reshape(tokens_here, attention_number, head_size).transpose(1, 0, 2)
-
-    queries = heads_first(normalize(
-        mixed_out[:, :, :per_group].reshape(tokens_here, attention_number, head_size)
-    ).astype(jnp.bfloat16))
-    key_unit = heads_first(normalize(
-        mixed_out[:, :, per_group : 2 * per_group].reshape(tokens_here, attention_number, head_size)
-    ).astype(jnp.bfloat16))
-    values = heads_first(mixed_out[:, :, 2 * per_group :].astype(jnp.bfloat16))
-    stacked = jnp.stack([key_unit, values], 0)[:, None]
+    wd = shortening_blocks(downsampling_filter, attention_number)
+    vmem = pl.BlockSpec(memory_space=pltpu.VMEM)
+    smem = pl.BlockSpec(memory_space=pltpu.SMEM)
+    queries, stacked = pl.pallas_call(
+        shorten_kernel,
+        out_shape=(
+            jax.ShapeDtypeStruct((attention_number, tokens_here, head_size), jnp.bfloat16),
+            jax.ShapeDtypeStruct((2, 1, attention_number, tokens_here, head_size), jnp.bfloat16),
+        ),
+        in_specs=[vmem, vmem, vmem],
+        out_specs=(vmem, vmem),
+        compiler_params=pltpu.CompilerParams(vmem_limit_bytes=60 * 1024 * 1024),
+    )(residual_stream, left_rim, wd)
     gathered = lax.all_gather(stacked, "seq", axis=1, tiled=True)
     my_index = lax.axis_index("seq").astype(jnp.int32).reshape(1)
     wup = widening_blocks(widening_filter, attention_number)
-    vmem = pl.BlockSpec(memory_space=pltpu.VMEM)
-    smem = pl.BlockSpec(memory_space=pltpu.SMEM)
     return pl.pallas_call(
         post_kernel,
         out_shape=jax.ShapeDtypeStruct((byte_rows, octet_readout.shape[0]), jnp.bfloat16),

time: 145 us -> 179 us (1.23)
  local copies, waits for them, and re-layouts: 23.9 us -> 54.6 us
  matrix products: 7.08 us -> 0 us
  Pallas kernels: 48.8 us -> 55.4 us
  other arithmetic: 5.72 us -> 7.79 us
    broadcast_in_dim x0 -> x6, local copies, waits for them, and re-layouts: none -> 34.8 us  [shortening_blocks(): blocks = jnp.where(eye, w, jnp.zeros((), w.dtype))]
    dot_general x1 -> x0, matrix products: 7.08 us -> none  [shorten(): jnp.einsum('jtgc,gtco->jgo', windows, kernel, preferred_element_type=jnp....]
    pallas_call x0 -> x1, Pallas kernels: none -> 6.85 us  [on_device(): pl.pallas_call(shorten_kernel, out_shape=(jax.ShapeDtypeStruct((attention...]
    select_n x0 -> x1, other arithmetic: none -> 6.28 us  [shortening_blocks(): blocks = jnp.where(eye, w, jnp.zeros((), w.dtype))]
    unnamed x7 -> x4, local copies, waits for them, and re-layouts: 3.88 us -> 0.61 us
    reshape x4 -> x1, local copies, waits for them, and re-layouts: 7.8 us -> 4.6 us  [shortening_blocks(): w = downsampling_filter.reshape(heads, gph, SHORTEN, width, 3, per_group)]
    transpose x0 -> x1, local copies, waits for them, and re-layouts: none -> 2.43 us  [shortening_blocks(): w = w.transpose(2, 0, 1, 3, 4, 5)[:, :, :, :, :, None, :]]
    concatenate x1 -> x0, other arithmetic: 1.88 us -> none  [on_device(): jnp.concatenate([left_rim, residual_stream[:byte_rows - rim_rows]], 0)]
  transfers between devices with their start and end apart: 2 -> 2, of which waited for: 1 -> 1; matrix products, arithmetic and copies ran while one was open for 12% -> 34% of each run, Pallas kernels for 0% -> 0%
where the time goes in v3:
time: 179 us; the launch traced here: 178 us
  Pallas kernels  55.4 us (31%)
  local copies, waits for them, and re-layouts  54.6 us (31%)
  waiting for transfers between devices  45.7 us (26%)
  between operations  13.5 us (8%)
  other arithmetic  7.79 us (4%)
    pallas_call x1, Pallas kernels, on_device(): pl.pallas_call(post_kernel, out_shape=jax.ShapeDtypeStruct((byte_rows, oc...  48.6 us
    all_gather x1, waiting for transfers between devices, on_device(): gathered = lax.all_gather(stacked, 'seq', axis=1, tiled=True)  45.7 us
    broadcast_in_dim x6, local copies, waits for them, and re-layouts, shortening_blocks(): blocks = jnp.where(eye, w, jnp.zeros((), w.dtype))  34.8 us
    broadcast_in_dim x4, local copies, waits for them, and re-layouts, widening_blocks(): blocks = jnp.where(eye, wf, jnp.zeros((), wf.dtype))  10.6 us
    pallas_call x1, Pallas kernels, on_device(): pl.pallas_call(shorten_kernel, out_shape=(jax.ShapeDtypeStruct((attention...  6.85 us
    select_n x1, other arithmetic, shortening_blocks(): blocks = jnp.where(eye, w, jnp.zeros((), w.dtype))  6.28 us
    reshape x1, local copies, waits for them, and re-layouts, shortening_blocks(): w = downsampling_filter.reshape(heads, gph, SHORTEN, width, 3, per_group)  4.6 us
  transfers between devices with their start and end apart: 2, of which 1 were waited for; matrix products, arithmetic and copies ran while one was open for 34% of the time, Pallas kernels for 0%

profile of v3, /device:TPU:449, one launch (start us, length us, event | category | flops | bytes accessed | tf_op | source)
XLA Modules:
  0.0 178.2 jit_solution(12681634820593901145)
XLA Ops:
  6.5 0.0 all-gather.2.cloned.1.call-start
  6.5 0.8 slice.3
  7.3 1.3 collective-permute-start
  8.6 4.6 %reshape.18 = bf16[8,4,4,64,3,32]{3,2,5,4,1,0:T(4,128)(2,1)S(1)} reshape(bf16[32,256,96]{1,2,0:T(8,128)(2,1)} %param.7) | data formatting | bytes 3145728 | tf_op jit(solution)/shard_map/reshape | solution.py:37
  13.2 2.4 %copy.9 = bf16[4,8,4,64,3,32]{3,2,5,4,1,0:T(4,128)(2,1)S(1)} copy(bf16[4,8,4,64,3,32]{3,0,5,4,2,1:T(4,128)(2,1)S(1)} %bitcast.9) | data formatting | bytes 3145728 | tf_op jit(solution)/shard_map/transpose | solution.py:38
  15.7 7.0 %broadcast_in_dim.59 = bf16[4,8,4,64,3,4,32]{3,2,6,5,4,1,0:T(4,128)(2,1)} broadcast(bf16[4,8,4,64,3,32]{3,2,5,4,1,0:T(4,128)(2,1)S(1)} %copy.9), dimensions={0,1,2,3,4,6} | broadcast | bytes 7864320 | tf_op jit(solution)/shard_map/jit(_where)/broadcast_in_dim | solution.py:40
  22.6 18.5 %broadcast_in_dim.60 = bf16[4,8,256,384]{2,3,1,0:T(8,128)(2,1)} reshape(bf16[4,8,4,64,3,4,32]{3,2,6,5,4,1,0:T(4,128)(2,1)} %broadcast_in_dim.59) | data formatting | bytes 12582912 | tf_op jit(solution)/shard_map/jit(_where)/broadcast_in_dim | solution.py:40
  41.1 8.6 %copy.10 = bf16[4,8,256,384]{3,2,1,0:T(8,128)(2,1)} copy(bf16[4,8,256,384]{2,3,1,0:T(8,128)(2,1)} %broadcast_in_dim.60) | data formatting | bytes 12582912 | tf_op jit(solution)/shard_map/jit(_where)/broadcast_in_dim | solution.py:40
  49.7 0.2 broadcast_in_dim.56
  49.9 0.3 broadcast_in_dim.57
  50.2 0.2 copy.8
  50.4 6.3 %broadcast_select_fusion.wd_ref = bf16[4,8,256,384]{3,2,1,0:T(8,128)(2,1)} fusion(bf16[4,8,256,384]{3,2,1,0:T(8,128)(2,1)} %copy.10, pred[256,384]{1,0:T(8,128)(4,1)S(1)} %copy.8), kind=kLoop, calls=%fused_computation | loop fusion | flops 3145728 | bytes 12681216 | tf_op jit(solution)/shard_map/jit(_where)/select_n | solution.py:40
  56.7 0.0 copy-start
  56.7 0.0 collective-permute-done.rim_ref
  56.7 0.0 copy-start.1
  56.7 0.6 copy-done.1
  57.3 6.8 %shard_map.55 = (bf16[8,128,128]{2,1,0:T(8,128)(2,1)}, bf16[2,1,8,128,128]{4,3,2,1,0:T(8,128)(2,1)}) custom-call(bf16[512,2048]{1,0:T(8,128)(2,1)} %res_ref.3, bf16[3,2048]{1,0:T(4,128)(2,1)} %copy-done.1, bf16[4,8,256,384]{3,2,1,0:T(8,128)(2,1)} %broadcast_select_fusion.wd_ref), custom_call_target="tpu_custom_call" | custom-call | tf_op jit(solution)/shard_map/pallas_call | solution.py:151
  64.2 0.0 all-gather.2.cloned.1.call-update
  64.2 0.1 copy.11
  64.3 0.0 copy-done
  64.3 0.4 reshape.19
  64.7 0.2 copy.12
  65.0 4.4 %broadcast_in_dim.65 = bf16[4,8,4,32,4,64]{5,4,3,2,1,0:T(4,128)(2,1)} broadcast(bf16[4,8,4,32,64]{4,3,2,1,0:T(8,128)(2,1)S(1)} %copy.12), dimensions={0,1,2,3,5} | broadcast | bytes 2621440 | tf_op jit(solution)/shard_map/jit(_where)/broadcast_in_dim | solution.py:28
  69.4 6.0 %broadcast_in_dim.66 = bf16[4,8,128,256]{3,2,1,0:T(8,128)(2,1)S(1)} reshape(bf16[4,8,4,32,4,64]{5,4,3,2,1,0:T(4,128)(2,1)} %broadcast_in_dim.65) | data formatting | bytes 4194304 | tf_op jit(solution)/shard_map/jit(_where)/broadcast_in_dim | solution.py:28
  75.4 0.1 broadcast_in_dim.62
  75.5 0.2 broadcast_in_dim.63
  75.6 1.5 broadcast_select_fusion.1.wup_ref
  77.1 45.7 %all-gather.2.cloned.1.call-done.kv_ref = bf16[2,16,8,128,128]{4,3,2,1,0:T(8,128)(2,1)} async-done(((bf16[2,1,8,128,128]{4,3,2,1,0:T(8,128)(2,1)}), bf16[2,16,8,128,128]{4,3,2,1,0:T(8,128)(2,1)}) %all-gather.2.cloned.1.call-update) | async-done | bytes 8388624 | tf_op jit(solution)/shard_map/all_gather | solution.py:161
  122.8 48.6 %shard_map.56 = bf16[512,256]{1,0:T(8,128)(2,1)} custom-call(s32[1]{0:T(128)} %bitcast.idx_ref, f32[8]{0:T(128)} %sharp_ref.1, bf16[8,128,128]{2,1,0:T(8,128)(2,1)} %get-tuple-element.7.q_ref, bf16[2,16,8,128,128]{4,3,2,1,0:T(8,128)(2,1)} %all-gather.2.cloned.1.call-done.kv_ref, bf16[4,8,128,256]{3,2,1,0:T(8,128)(2,1)} %broadcast_select_fusion.1.wup_ref, ...), custom_call_target="tpu_custom_call" | custom-call | tf_op jit(solution)/shard_map/pallas_call | solution.py:164
  (1 shorter events, 0.0 us)
Async XLA Ops:
  6.5 116.2 %all-gather.2.cloned.1.call-start = ((), (), s32[]{:S(2)}) async-start(), calls=%async_computation | async-start | bytes 8912896 | tf_op jit(solution)/shard_map/all_gather | solution.py:161
  7.3 49.4 %collective-permute-start = (bf16[3,2048]{1,0:T(4,128)(2,1)S(1)}, bf16[3,2048]{1,0:T(4,128)(2,1)S(1)}, u32[]{:S(2)}, u32[]{:S(2)}) collective-permute-start(bf16[3,2048]{1,0:T(4,128)(2,1)S(1)} %slice.3), channel_id=1, source_target_pairs={{0,1},{1,2},{2,3},{3,4},{4,5},{5,6},{6,7},{7,8},{8,9},{9,10},{10,1... | collective-permute-start | bytes 36872 | tf_op jit(solution)/shard_map/ppermute | solution.py:14
  56.7 7.6 %copy-start = (bf16[32,32,256]{2,1,0:T(8,128)(2,1)S(1)}, bf16[32,32,256]{2,1,0:T(8,128)(2,1)}, u32[]{:S(2)}) copy-start(bf16[32,32,256]{2,1,0:T(8,128)(2,1)} %param.9) | copy-start | bytes 1572868
  56.7 0.6 copy-start.1
Sparse Core Ops, SparseCore 0:
  64.3 58.4 all-gather.1

commit v4 on v3

--- a/solution.py
+++ b/solution.py
@@ -29,25 +29,16 @@
     return blocks.reshape(SHORTEN, heads, gph * per_group, gph * width)
 
 
-def shortening_blocks(downsampling_filter, heads):
-    groups, span, outs = downsampling_filter.shape
-    gph = groups // heads
-    width = span // SHORTEN
-    per_group = outs // 3
-    w = downsampling_filter.reshape(heads, gph, SHORTEN, width, 3, per_group)
-    w = w.transpose(2, 0, 1, 3, 4, 5)[:, :, :, :, :, None, :]
-    eye = jnp.eye(gph, dtype=jnp.bool_)[:, None, None, :, None]
-    blocks = jnp.where(eye, w, jnp.zeros((), w.dtype))
-    return blocks.reshape(SHORTEN, heads, gph * width, 3 * gph * per_group)
-
-
 def shorten_kernel(res_ref, rim_ref, wd_ref, q_ref, kv_ref):
     f32, bf16 = jnp.float32, jnp.bfloat16
     rows = res_ref.shape[0]
     tokens = rows // SHORTEN
-    heads = wd_ref.shape[1]
-    cin = wd_ref.shape[2]
-    hd = wd_ref.shape[3] // 3
+    heads = q_ref.shape[0]
+    hd = q_ref.shape[2]
+    groups, span, outs = wd_ref.shape
+    gph = groups // heads
+    width = span // SHORTEN
+    per_group = outs // 3
     j_i = lax.broadcasted_iota(jnp.int32, (tokens, rows), 0)
     r_i = lax.broadcasted_iota(jnp.int32, (tokens, rows), 1)
     first = lax.broadcasted_iota(jnp.int32, (tokens, 1), 0) == 0
@@ -59,15 +50,28 @@
         if t < SHORTEN - 1:
             x = jnp.where(first, rim_ref[pl.ds(t, 1), :], x)
         picked.append(x)
+    i_i = lax.broadcasted_iota(jnp.int32, (outs, 3 * hd), 0)
+    n_i = lax.broadcasted_iota(jnp.int32, (outs, 3 * hd), 1)
+    place = [
+        (n_i == (i_i // per_group) * hd + g * per_group + i_i % per_group).astype(bf16)
+        for g in range(gph)
+    ]
+    pair = 128 // width
     for k in range(heads):
         acc = None
-        for t in range(SHORTEN):
-            part = jnp.dot(picked[t][:, k * cin : (k + 1) * cin], wd_ref[t, k], preferred_element_type=f32)
-            acc = part if acc is None else acc + part
-        q = acc[:, :hd]
-        key = acc[:, hd : 2 * hd]
-        q_ref[k] = normalize(q).astype(bf16)
-        kv_ref[0, 0, k] = normalize(key).astype(bf16)
+        for m in range(gph // pair):
+            for t in range(SHORTEN):
+                pieces = []
+                for e in range(pair):
+                    g = m * pair + e
+                    w = wd_ref[k * gph + g, pl.ds(t * width, width), :]
+                    pieces.append(jnp.dot(w, place[g], preferred_element_type=f32).astype(bf16))
+                wp = jnp.concatenate(pieces, axis=0)
+                col = (k * gph + m * pair) * width
+                part = jnp.dot(picked[t][:, col : col + 128], wp, preferred_element_type=f32)
+                acc = part if acc is None else acc + part
+        q_ref[k] = normalize(acc[:, :hd]).astype(bf16)
+        kv_ref[0, 0, k] = normalize(acc[:, hd : 2 * hd]).astype(bf16)
         kv_ref[1, 0, k] = acc[:, 2 * hd :].astype(bf16)
 
 
@@ -75,25 +79,19 @@
     me = idx_ref[0]
     heads, tq, hd = q_ref.shape
     f32, bf16 = jnp.float32, jnp.bfloat16
-    qpos = me * tq + lax.broadcasted_iota(jnp.int32, (tq, tq), 0)
-    kio = lax.broadcasted_iota(jnp.int32, (tq, tq), 1)
+    nb = kv_ref.shape[1]
+    qpos = me * tq + lax.broadcasted_iota(jnp.int32, (tq, nb * tq), 0)
+    kpos = lax.broadcasted_iota(jnp.int32, (tq, nb * tq), 1)
+    visible = kpos <= qpos
     for h in range(heads):
         q = q_ref[h]
         sharp = sharp_ref[h]
-
-        def body(d, carry, q=q, sharp=sharp, h=h):
-            num, den = carry
-            s = lax.dot_general(
-                q, kv_ref[0, d, h], (((1,), (1,)), ((), ())), preferred_element_type=f32
-            ) * sharp
-            w = jnp.where(d * tq + kio <= qpos, jnp.exp(s - sharp), jnp.zeros((), f32))
-            den = den + jnp.sum(w, axis=1, keepdims=True)
-            num = num + jnp.dot(w.astype(bf16), kv_ref[1, d, h], preferred_element_type=f32)
-            return num, den
-
-        num, den = lax.fori_loop(
-            0, me + 1, body, (jnp.zeros((tq, hd), f32), jnp.zeros((tq, 1), f32))
-        )
+        keys = jnp.concatenate([kv_ref[0, d, h] for d in range(nb)], axis=0)
+        vals = jnp.concatenate([kv_ref[1, d, h] for d in range(nb)], axis=0)
+        s = lax.dot_general(q, keys, (((1,), (1,)), ((), ())), preferred_element_type=f32) * sharp
+        w = jnp.where(visible, jnp.exp(s - sharp), jnp.zeros((), f32))
+        den = jnp.sum(w, axis=1, keepdims=True)
+        num = jnp.dot(w.astype(bf16), vals, preferred_element_type=f32)
         att_scr[:, h * hd : (h + 1) * hd] = (num / den).astype(bf16)
 
     rows, width = res_ref.shape
@@ -145,7 +143,6 @@
     tokens_here = byte_rows // SHORTEN
     rim_rows = SHORTEN - 1
     left_rim = shifted_2(residual_stream[byte_rows - rim_rows :], "seq", 1)
-    wd = shortening_blocks(downsampling_filter, attention_number)
     vmem = pl.BlockSpec(memory_space=pltpu.VMEM)
     smem = pl.BlockSpec(memory_space=pltpu.SMEM)
     queries, stacked = pl.pallas_call(
@@ -157,7 +154,7 @@
         in_specs=[vmem, vmem, vmem],
         out_specs=(vmem, vmem),
         compiler_params=pltpu.CompilerParams(vmem_limit_bytes=60 * 1024 * 1024),
-    )(residual_stream, left_rim, wd)
+    )(residual_stream, left_rim, downsampling_filter)
     gathered = lax.all_gather(stacked, "seq", axis=1, tiled=True)
     my_index = lax.axis_index("seq").astype(jnp.int32).reshape(1)
     wup = widening_blocks(widening_filter, attention_number)

time: 179 us -> 118 us (0.66)
  the two profiles are of different devices: /device:TPU:449 before, /device:TPU:6 now
where the time goes in v4:
time: 118 us; the launch traced here: 116 us
  waiting for transfers between devices  52.4 us (44%)
  Pallas kernels  30.3 us (26%)
  local copies, waits for them, and re-layouts  16.7 us (14%)
  between operations  13.5 us (11%)
  starting transfers between devices  1.74 us (1%)
  other arithmetic  1.51 us (1%)
    all_gather x1, waiting for transfers between devices, on_device(): gathered = lax.all_gather(stacked, 'seq', axis=1, tiled=True)  52.4 us
    pallas_call x1, Pallas kernels, on_device(): pl.pallas_call(shorten_kernel, out_shape=(jax.ShapeDtypeStruct((attention...  15.5 us
    pallas_call x1, Pallas kernels, on_device(): pl.pallas_call(post_kernel, out_shape=jax.ShapeDtypeStruct((byte_rows, oc...  14.8 us
    broadcast_in_dim x4, local copies, waits for them, and re-layouts, widening_blocks(): blocks = jnp.where(eye, wf, jnp.zeros((), wf.dtype))  10.8 us
    unnamed x5, local copies, waits for them, and re-layouts  4.47 us
  transfers between devices with their start and end apart: 2, of which 1 were waited for; matrix products, arithmetic and copies ran while one was open for 14% of the time, Pallas kernels for 0%

profile of v4, /device:TPU:6, one launch (start us, length us, event | category | flops | bytes accessed | tf_op | source)
XLA Modules:
  0.0 116.1 jit_solution(2680278191485520752)
XLA Ops:
  6.5 0.0 all-gather.2.cloned.1.call-start
  6.5 0.8 slice.3
  7.3 1.7 %collective-permute-start = (bf16[3,2048]{1,0:T(4,128)(2,1)S(1)}, bf16[3,2048]{1,0:T(4,128)(2,1)S(1)}, u32[]{:S(2)}, u32[]{:S(2)}) collective-permute-start(bf16[3,2048]{1,0:T(4,128)(2,1)S(1)} %slice.3), channel_id=1, source_target_pairs={{0,1},{1,2},{2,3},{3,4},{4,5},{5,6},{6,7},{7,8},{8,9},{9,10},{10,1... | collective-permute-start | bytes 36872 | tf_op jit(solution)/shard_map/ppermute | solution.py:14
  9.1 3.9 %copy.6.wd_ref = bf16[32,256,96]{2,1,0:T(8,128)(2,1)} copy(bf16[32,256,96]{1,2,0:T(8,128)(2,1)} %param.7) | data formatting | bytes 3145728 | tf_op args[2]
  12.9 0.0 copy-start
  12.9 0.0 collective-permute-done.rim_ref
  12.9 0.0 copy-start.1
  12.9 0.6 copy-done.1
  13.5 15.5 %shard_map.55 = (bf16[8,128,128]{2,1,0:T(8,128)(2,1)}, bf16[2,1,8,128,128]{4,3,2,1,0:T(8,128)(2,1)}) custom-call(bf16[512,2048]{1,0:T(8,128)(2,1)} %res_ref.3, bf16[3,2048]{1,0:T(4,128)(2,1)} %copy-done.1, bf16[32,256,96]{2,1,0:T(8,128)(2,1)} %copy.6.wd_ref), custom_call_target="tpu_custom_call" | custom-call | tf_op jit(solution)/shard_map/pallas_call | solution.py:148
  29.0 0.0 all-gather.2.cloned.1.call-update
  29.1 0.0 copy-done
  29.1 0.4 reshape.11
  29.5 0.2 copy.7
  29.7 4.4 %broadcast_in_dim.31 = bf16[4,8,4,32,4,64]{5,4,3,2,1,0:T(4,128)(2,1)} broadcast(bf16[4,8,4,32,64]{4,3,2,1,0:T(8,128)(2,1)S(1)} %copy.7), dimensions={0,1,2,3,5} | broadcast | bytes 2621440 | tf_op jit(solution)/shard_map/jit(_where)/broadcast_in_dim | solution.py:28
  34.1 6.1 %broadcast_in_dim.32 = bf16[4,8,128,256]{3,2,1,0:T(8,128)(2,1)S(1)} reshape(bf16[4,8,4,32,4,64]{5,4,3,2,1,0:T(4,128)(2,1)} %broadcast_in_dim.31) | data formatting | bytes 4194304 | tf_op jit(solution)/shard_map/jit(_where)/broadcast_in_dim | solution.py:28
  40.3 0.1 broadcast_in_dim.28
  40.4 0.2 broadcast_in_dim.29
  40.6 1.5 %broadcast_select_fusion.wup_ref = bf16[4,8,128,256]{3,2,1,0:T(8,128)(2,1)} fusion(bf16[4,8,128,256]{3,2,1,0:T(8,128)(2,1)S(1)} %broadcast_in_dim.32, pred[128,256]{1,0:T(8,128)(4,1)S(1)} %broadcast_in_dim.29), kind=kLoop, calls=%fused_computation | loop fusion | flops 1048576 | bytes 4227072 | tf_op jit(solution)/shard_map/jit(_where)/select_n | solution.py:28
  42.1 52.4 %all-gather.2.cloned.1.call-done.kv_ref = bf16[2,16,8,128,128]{4,3,2,1,0:T(8,128)(2,1)} async-done(((bf16[2,1,8,128,128]{4,3,2,1,0:T(8,128)(2,1)}), bf16[2,16,8,128,128]{4,3,2,1,0:T(8,128)(2,1)}) %all-gather.2.cloned.1.call-update) | async-done | bytes 8388624 | tf_op jit(solution)/shard_map/all_gather | solution.py:158
  94.5 14.8 %shard_map.56 = bf16[512,256]{1,0:T(8,128)(2,1)} custom-call(s32[1]{0:T(128)} %bitcast.idx_ref, f32[8]{0:T(128)} %sharp_ref.1, bf16[8,128,128]{2,1,0:T(8,128)(2,1)} %get-tuple-element.7.q_ref, bf16[2,16,8,128,128]{4,3,2,1,0:T(8,128)(2,1)} %all-gather.2.cloned.1.call-done.kv_ref, bf16[4,8,128,256]{3,2,1,0:T(8,128)(2,1)} %broadcast_select_fusion.wup_ref, ...), custom_call_target="tpu_custom_call" | custom-call | tf_op jit(solution)/shard_map/pallas_call | solution.py:161
  (1 shorter events, 0.0 us)
Async XLA Ops:
  6.5 87.9 %all-gather.2.cloned.1.call-start = ((), (), s32[]{:S(2)}) async-start(), calls=%async_computation | async-start | bytes 8912896 | tf_op jit(solution)/shard_map/all_gather | solution.py:158
  7.3 5.6 %collective-permute-start = (bf16[3,2048]{1,0:T(4,128)(2,1)S(1)}, bf16[3,2048]{1,0:T(4,128)(2,1)S(1)}, u32[]{:S(2)}, u32[]{:S(2)}) collective-permute-start(bf16[3,2048]{1,0:T(4,128)(2,1)S(1)} %slice.3), channel_id=1, source_target_pairs={{0,1},{1,2},{2,3},{3,4},{4,5},{5,6},{6,7},{7,8},{8,9},{9,10},{10,1... | collective-permute-start | bytes 36872 | tf_op jit(solution)/shard_map/ppermute | solution.py:14
  12.9 16.1 %copy-start = (bf16[32,32,256]{2,1,0:T(8,128)(2,1)S(1)}, bf16[32,32,256]{2,1,0:T(8,128)(2,1)}, u32[]{:S(2)}) copy-start(bf16[32,32,256]{2,1,0:T(8,128)(2,1)} %param.9) | copy-start | bytes 1572868
  12.9 0.6 copy-start.1
Sparse Core Ops, SparseCore 0:
  29.2 65.2 all-gather.1

commit v5 on v4

--- a/solution.py
+++ b/solution.py
@@ -1,3 +1,5 @@
+import functools
+
 import jax
 import jax.numpy as jnp
 from jax import lax
@@ -29,16 +31,16 @@
     return blocks.reshape(SHORTEN, heads, gph * per_group, gph * width)
 
 
-def shorten_kernel(res_ref, rim_ref, wd_ref, q_ref, kv_ref):
+def shorten_kernel(res_ref, rim_ref, wd_ref, q_ref, kv_ref, *, head0):
     f32, bf16 = jnp.float32, jnp.bfloat16
     rows = res_ref.shape[0]
     tokens = rows // SHORTEN
     heads = q_ref.shape[0]
     hd = q_ref.shape[2]
     groups, span, outs = wd_ref.shape
-    gph = groups // heads
     width = span // SHORTEN
     per_group = outs // 3
+    gph = hd // per_group
     j_i = lax.broadcasted_iota(jnp.int32, (tokens, rows), 0)
     r_i = lax.broadcasted_iota(jnp.int32, (tokens, rows), 1)
     first = lax.broadcasted_iota(jnp.int32, (tokens, 1), 0) == 0
@@ -57,7 +59,8 @@
         for g in range(gph)
     ]
     pair = 128 // width
-    for k in range(heads):
+    for kk in range(heads):
+        k = head0 + kk
         acc = None
         for m in range(gph // pair):
             for t in range(SHORTEN):
@@ -70,29 +73,40 @@
                 col = (k * gph + m * pair) * width
                 part = jnp.dot(picked[t][:, col : col + 128], wp, preferred_element_type=f32)
                 acc = part if acc is None else acc + part
-        q_ref[k] = normalize(acc[:, :hd]).astype(bf16)
-        kv_ref[0, 0, k] = normalize(acc[:, hd : 2 * hd]).astype(bf16)
-        kv_ref[1, 0, k] = acc[:, 2 * hd :].astype(bf16)
-
-
-def post_kernel(idx_ref, sharp_ref, q_ref, kv_ref, wup_ref, res_ref, oct_ref, out_ref, att_scr):
-    me = idx_ref[0]
+        q_ref[kk] = normalize(acc[:, :hd]).astype(bf16)
+        kv_ref[0, 0, kk] = normalize(acc[:, hd : 2 * hd]).astype(bf16)
+        kv_ref[1, 0, kk] = acc[:, 2 * hd :].astype(bf16)
+
+
+def attend_heads(me, sharp_ref, head0, q_ref, kv_ref, att_ref, col0):
+    f32, bf16 = jnp.float32, jnp.bfloat16
     heads, tq, hd = q_ref.shape
-    f32, bf16 = jnp.float32, jnp.bfloat16
     nb = kv_ref.shape[1]
     qpos = me * tq + lax.broadcasted_iota(jnp.int32, (tq, nb * tq), 0)
     kpos = lax.broadcasted_iota(jnp.int32, (tq, nb * tq), 1)
     visible = kpos <= qpos
     for h in range(heads):
         q = q_ref[h]
-        sharp = sharp_ref[h]
+        sharp = sharp_ref[head0 + h]
         keys = jnp.concatenate([kv_ref[0, d, h] for d in range(nb)], axis=0)
         vals = jnp.concatenate([kv_ref[1, d, h] for d in range(nb)], axis=0)
         s = lax.dot_general(q, keys, (((1,), (1,)), ((), ())), preferred_element_type=f32) * sharp
         w = jnp.where(visible, jnp.exp(s - sharp), jnp.zeros((), f32))
         den = jnp.sum(w, axis=1, keepdims=True)
         num = jnp.dot(w.astype(bf16), vals, preferred_element_type=f32)
-        att_scr[:, h * hd : (h + 1) * hd] = (num / den).astype(bf16)
+        att_ref[:, col0 + h * hd : col0 + (h + 1) * hd] = (num / den).astype(bf16)
+
+
+def first_kernel(idx_ref, sharp_ref, q_ref, kv_ref, att_ref):
+    attend_heads(idx_ref[0], sharp_ref, 0, q_ref, kv_ref, att_ref, 0)
+
+
+def post_kernel(idx_ref, sharp_ref, q_ref, kv_ref, early_ref, wup_ref, res_ref, oct_ref, out_ref, att_scr):
+    f32, bf16 = jnp.float32, jnp.bfloat16
+    done = early_ref.shape[1]
+    heads_done = sharp_ref.shape[0] - q_ref.shape[0]
+    att_scr[:, :done] = early_ref[...]
+    attend_heads(idx_ref[0], sharp_ref, heads_done, q_ref, kv_ref, att_scr, done)
 
     rows, width = res_ref.shape
     row_blocks = rows // 128
@@ -145,27 +159,42 @@
     left_rim = shifted_2(residual_stream[byte_rows - rim_rows :], "seq", 1)
     vmem = pl.BlockSpec(memory_space=pltpu.VMEM)
     smem = pl.BlockSpec(memory_space=pltpu.SMEM)
-    queries, stacked = pl.pallas_call(
-        shorten_kernel,
-        out_shape=(
-            jax.ShapeDtypeStruct((attention_number, tokens_here, head_size), jnp.bfloat16),
-            jax.ShapeDtypeStruct((2, 1, attention_number, tokens_here, head_size), jnp.bfloat16),
-        ),
-        in_specs=[vmem, vmem, vmem],
-        out_specs=(vmem, vmem),
-        compiler_params=pltpu.CompilerParams(vmem_limit_bytes=60 * 1024 * 1024),
-    )(residual_stream, left_rim, downsampling_filter)
-    gathered = lax.all_gather(stacked, "seq", axis=1, tiled=True)
+    params = pltpu.CompilerParams(vmem_limit_bytes=60 * 1024 * 1024)
+    half = attention_number // 2
     my_index = lax.axis_index("seq").astype(jnp.int32).reshape(1)
+
+    def shorten_half(head0):
+        return pl.pallas_call(
+            functools.partial(shorten_kernel, head0=head0),
+            out_shape=(
+                jax.ShapeDtypeStruct((half, tokens_here, head_size), jnp.bfloat16),
+                jax.ShapeDtypeStruct((2, 1, half, tokens_here, head_size), jnp.bfloat16),
+            ),
+            in_specs=[vmem, vmem, vmem],
+            out_specs=(vmem, vmem),
+            compiler_params=params,
+        )(residual_stream, left_rim, downsampling_filter)
+
+    q_a, kv_a = shorten_half(0)
+    gathered_a = lax.all_gather(kv_a, "seq", axis=1, tiled=True)
+    q_b, kv_b = shorten_half(half)
+    gathered_b = lax.all_gather(kv_b, "seq", axis=1, tiled=True)
+    early = pl.pallas_call(
+        first_kernel,
+        out_shape=jax.ShapeDtypeStruct((tokens_here, half * head_size), jnp.bfloat16),
+        in_specs=[smem, smem, vmem, vmem],
+        out_specs=vmem,
+        compiler_params=params,
+    )(my_index, sharpness_factor, q_a, gathered_a)
     wup = widening_blocks(widening_filter, attention_number)
     return pl.pallas_call(
         post_kernel,
         out_shape=jax.ShapeDtypeStruct((byte_rows, octet_readout.shape[0]), jnp.bfloat16),
-        in_specs=[smem, smem, vmem, vmem, vmem, vmem, vmem],
+        in_specs=[smem, smem, vmem, vmem, vmem, vmem, vmem, vmem],
         out_specs=vmem,
         scratch_shapes=[pltpu.VMEM((tokens_here, attention_number * head_size), jnp.bfloat16)],
-        compiler_params=pltpu.CompilerParams(vmem_limit_bytes=60 * 1024 * 1024),
-    )(my_index, sharpness_factor, queries, gathered, wup, residual_stream, octet_readout)
+        compiler_params=params,
+    )(my_index, sharpness_factor, q_b, gathered_b, early, wup, residual_stream, octet_readout)
 
 
 def solution(mesh):

time: 118 us -> 140 us (1.19)
  waiting for transfers between devices: 52.4 us -> 69.5 us
  Pallas kernels: 30.3 us -> 35.6 us
    all_gather x1 -> x2, waiting for transfers between devices: 52.4 us -> 69.4 us  [the longest x1 40.4 us: on_device(): gathered_b = lax.all_gather(kv_b, 'seq', axis=1, tiled=True)]
    pallas_call x1 -> x3, Pallas kernels: 15.5 us -> 23.5 us  [the longest x2 18.7 us: shorten_half(): pl.pallas_call(functools.partial(shorten_kernel, head0=head0), out_shape=...]
    pallas_call x1, Pallas kernels: 14.8 us -> 12.1 us  [on_device(): pl.pallas_call(post_kernel, out_shape=jax.ShapeDtypeStruct((byte_rows, oc...]
  transfers between devices with their start and end apart: 2 -> 3, of which waited for: 1 -> 2; matrix products, arithmetic and copies ran while one was open for 14% -> 12% of each run, Pallas kernels for 0% -> 10%
where the time goes in v5:
time: 140 us; the launch traced here: 138 us
  waiting for transfers between devices  69.5 us (50%)
  Pallas kernels  35.6 us (25%)
  local copies, waits for them, and re-layouts  16.5 us (12%)
  between operations  13.5 us (10%)
  starting transfers between devices  1.78 us (1%)
  other arithmetic  1.51 us (1%)
    all_gather x1, waiting for transfers between devices, on_device(): gathered_b = lax.all_gather(kv_b, 'seq', axis=1, tiled=True)  40.4 us
    all_gather x1, waiting for transfers between devices, on_device(): gathered_a = lax.all_gather(kv_a, 'seq', axis=1, tiled=True)  29.1 us
    pallas_call x2, Pallas kernels, shorten_half(): pl.pallas_call(functools.partial(shorten_kernel, head0=head0), out_shape=...  18.7 us
    pallas_call x1, Pallas kernels, on_device(): pl.pallas_call(post_kernel, out_shape=jax.ShapeDtypeStruct((byte_rows, oc...  12.1 us
    broadcast_in_dim x4, local copies, waits for them, and re-layouts, widening_blocks(): blocks = jnp.where(eye, wf, jnp.zeros((), wf.dtype))  10.6 us
    pallas_call x1, Pallas kernels, on_device(): pl.pallas_call(first_kernel, out_shape=jax.ShapeDtypeStruct((tokens_here,...  4.86 us
    unnamed x5, local copies, waits for them, and re-layouts  4.45 us
  transfers between devices with their start and end apart: 3, of which 2 were waited for; matrix products, arithmetic and copies ran while one was open for 12% of the time, Pallas kernels for 10%

profile of v5, /device:TPU:6, one launch (start us, length us, event | category | flops | bytes accessed | tf_op | source)
XLA Modules:
  0.0 138.3 jit_solution(17715902690516755508)
XLA Ops:
  6.5 0.0 all-gather.5.cloned.1.call-start
  6.5 0.8 slice.3
  7.3 1.7 %collective-permute-start = (bf16[3,2048]{1,0:T(4,128)(2,1)S(1)}, bf16[3,2048]{1,0:T(4,128)(2,1)S(1)}, u32[]{:S(2)}, u32[]{:S(2)}) collective-permute-start(bf16[3,2048]{1,0:T(4,128)(2,1)S(1)} %slice.3), channel_id=1, source_target_pairs={{0,1},{1,2},{2,3},{3,4},{4,5},{5,6},{6,7},{7,8},{8,9},{9,10},{10,1... | collective-permute-start | bytes 36872 | tf_op jit(solution)/shard_map/ppermute | solution.py:16
  9.1 3.8 %copy.6.wd_ref = bf16[32,256,96]{2,1,0:T(8,128)(2,1)} copy(bf16[32,256,96]{1,2,0:T(8,128)(2,1)} %param.7) | data formatting | bytes 3145728 | tf_op args[2]
  12.9 0.0 collective-permute-done.rim_ref
  12.9 0.0 copy-start.1
  12.9 0.6 copy-done.1
  13.5 9.3 %shard_map.56 = (bf16[4,128,128]{2,1,0:T(8,128)(2,1)}, bf16[2,1,4,128,128]{4,3,2,1,0:T(8,128)(2,1)}) custom-call(bf16[512,2048]{1,0:T(8,128)(2,1)} %res_ref.5, bf16[3,2048]{1,0:T(4,128)(2,1)} %copy-done.1, bf16[32,256,96]{2,1,0:T(8,128)(2,1)} %copy.6.wd_ref), custom_call_target="tpu_custom_call" | custom-call | tf_op jit(solution)/shard_map/pallas_call | solution.py:167
  22.8 0.0 all-gather.5.cloned.1.call-update
  22.8 0.0 copy-start
  22.9 0.0 all-gather.3.cloned.1.call-start
  22.9 9.4 %shard_map.55 = (bf16[4,128,128]{2,1,0:T(8,128)(2,1)}, bf16[2,1,4,128,128]{4,3,2,1,0:T(8,128)(2,1)}) custom-call(bf16[512,2048]{1,0:T(8,128)(2,1)} %res_ref.5, bf16[3,2048]{1,0:T(4,128)(2,1)} %copy-done.1, bf16[32,256,96]{2,1,0:T(8,128)(2,1)} %copy.6.wd_ref), custom_call_target="tpu_custom_call" | custom-call | tf_op jit(solution)/shard_map/pallas_call | solution.py:167
  32.3 0.0 all-gather.3.cloned.1.call-update
  32.3 0.0 copy-done
  32.3 0.4 reshape.11
  32.7 0.2 copy.8
  33.0 4.4 %broadcast_in_dim.31 = bf16[4,8,4,32,4,64]{5,4,3,2,1,0:T(4,128)(2,1)} broadcast(bf16[4,8,4,32,64]{4,3,2,1,0:T(8,128)(2,1)S(1)} %copy.8), dimensions={0,1,2,3,5} | broadcast | bytes 2621440 | tf_op jit(solution)/shard_map/jit(_where)/broadcast_in_dim | solution.py:30
  37.4 6.0 %broadcast_in_dim.32 = bf16[4,8,128,256]{3,2,1,0:T(8,128)(2,1)S(1)} reshape(bf16[4,8,4,32,4,64]{5,4,3,2,1,0:T(4,128)(2,1)} %broadcast_in_dim.31) | data formatting | bytes 4194304 | tf_op jit(solution)/shard_map/jit(_where)/broadcast_in_dim | solution.py:30
  43.3 0.1 broadcast_in_dim.28
  43.5 0.2 broadcast_in_dim.29
  43.6 1.5 %broadcast_select_fusion.wup_ref = bf16[4,8,128,256]{3,2,1,0:T(8,128)(2,1)} fusion(bf16[4,8,128,256]{3,2,1,0:T(8,128)(2,1)S(1)} %broadcast_in_dim.32, pred[128,256]{1,0:T(8,128)(4,1)S(1)} %broadcast_in_dim.29), kind=kLoop, calls=%fused_computation | loop fusion | flops 1048576 | bytes 4227072 | tf_op jit(solution)/shard_map/jit(_where)/select_n | solution.py:30
  45.1 29.1 %all-gather.5.cloned.1.call-done.kv_ref = bf16[2,16,4,128,128]{4,3,2,1,0:T(8,128)(2,1)} async-done(((bf16[2,1,4,128,128]{4,3,2,1,0:T(8,128)(2,1)}), bf16[2,16,4,128,128]{4,3,2,1,0:T(8,128)(2,1)}) %all-gather.5.cloned.1.call-update) | async-done | bytes 4194320 | tf_op jit(solution)/shard_map/all_gather | solution.py:179
  74.2 4.9 %shard_map.57.early_ref = bf16[128,512]{1,0:T(8,128)(2,1)} custom-call(s32[1]{0:T(128)} %bitcast.idx_ref, f32[8]{0:T(128)} %sharp_ref.3, bf16[4,128,128]{2,1,0:T(8,128)(2,1)} %get-tuple-element.11.q_ref, bf16[2,16,4,128,128]{4,3,2,1,0:T(8,128)(2,1)} %all-gather.5.cloned.1.call-done.kv_ref), custom_call_target="tpu_custom_call" | custom-call | tf_op jit(solution)/shard_map/pallas_call | solution.py:182
  79.0 40.4 %all-gather.3.cloned.1.call-done.kv_ref = bf16[2,16,4,128,128]{4,3,2,1,0:T(8,128)(2,1)} async-done(((bf16[2,1,4,128,128]{4,3,2,1,0:T(8,128)(2,1)}), bf16[2,16,4,128,128]{4,3,2,1,0:T(8,128)(2,1)}) %all-gather.3.cloned.1.call-update) | async-done | bytes 4194320 | tf_op jit(solution)/shard_map/all_gather | solution.py:181
  119.4 12.1 %shard_map.58 = bf16[512,256]{1,0:T(8,128)(2,1)} custom-call(s32[1]{0:T(128)} %bitcast.idx_ref, f32[8]{0:T(128)} %sharp_ref.3, bf16[4,128,128]{2,1,0:T(8,128)(2,1)} %get-tuple-element.9.q_ref, bf16[2,16,4,128,128]{4,3,2,1,0:T(8,128)(2,1)} %all-gather.3.cloned.1.call-done.kv_ref, bf16[128,512]{1,0:T(8,128)(2,1)} %shard_map.57.early_ref, ...), custom_call_target="tpu_custom_call" | custom-call | tf_op jit(solution)/shard_map/pallas_call | solution.py:190
  (1 shorter events, 0.0 us)
Async XLA Ops:
  6.5 67.6 %all-gather.5.cloned.1.call-start = ((), (), s32[]{:S(2)}) async-start(), calls=%async_computation.1 | async-start | bytes 4456448 | tf_op jit(solution)/shard_map/all_gather | solution.py:179
  7.3 5.6 %collective-permute-start = (bf16[3,2048]{1,0:T(4,128)(2,1)S(1)}, bf16[3,2048]{1,0:T(4,128)(2,1)S(1)}, u32[]{:S(2)}, u32[]{:S(2)}) collective-permute-start(bf16[3,2048]{1,0:T(4,128)(2,1)S(1)} %slice.3), channel_id=1, source_target_pairs={{0,1},{1,2},{2,3},{3,4},{4,5},{5,6},{6,7},{7,8},{8,9},{9,10},{10,1... | collective-permute-start | bytes 36872 | tf_op jit(solution)/shard_map/ppermute | solution.py:16
  12.9 0.6 copy-start.1
  22.8 9.4 %copy-start = (bf16[32,32,256]{2,1,0:T(8,128)(2,1)S(1)}, bf16[32,32,256]{2,1,0:T(8,128)(2,1)}, u32[]{:S(2)}) copy-start(bf16[32,32,256]{2,1,0:T(8,128)(2,1)} %param.9) | copy-start | bytes 1572868
  22.9 96.6 %all-gather.3.cloned.1.call-start = ((), (), s32[]{:S(2)}) async-start(), calls=%async_computation | async-start | bytes 4456448 | tf_op jit(solution)/shard_map/all_gather | solution.py:181
Sparse Core Ops, SparseCore 0:
  23.0 51.1 all-gather.4
  76.3 43.0 all-gather.2

commit v6 on v4

--- a/solution.py
+++ b/solution.py
@@ -1,3 +1,5 @@
+import functools
+
 import jax
 import jax.numpy as jnp
 from jax import lax
@@ -29,16 +31,16 @@
     return blocks.reshape(SHORTEN, heads, gph * per_group, gph * width)
 
 
-def shorten_kernel(res_ref, rim_ref, wd_ref, q_ref, kv_ref):
+def shorten_kernel(res_ref, rim_ref, wd_ref, *outs, parts):
     f32, bf16 = jnp.float32, jnp.bfloat16
     rows = res_ref.shape[0]
     tokens = rows // SHORTEN
-    heads = q_ref.shape[0]
-    hd = q_ref.shape[2]
-    groups, span, outs = wd_ref.shape
+    heads = outs[0].shape[-3]
+    hd = outs[0].shape[-1]
+    groups, span, channels = wd_ref.shape
     gph = groups // heads
     width = span // SHORTEN
-    per_group = outs // 3
+    per_group = channels // 3
     j_i = lax.broadcasted_iota(jnp.int32, (tokens, rows), 0)
     r_i = lax.broadcasted_iota(jnp.int32, (tokens, rows), 1)
     first = lax.broadcasted_iota(jnp.int32, (tokens, 1), 0) == 0
@@ -50,8 +52,10 @@
         if t < SHORTEN - 1:
             x = jnp.where(first, rim_ref[pl.ds(t, 1), :], x)
         picked.append(x)
-    i_i = lax.broadcasted_iota(jnp.int32, (outs, 3 * hd), 0)
-    n_i = lax.broadcasted_iota(jnp.int32, (outs, 3 * hd), 1)
+    first_part = 0 if parts == "q" else 1
+    n_parts = 1 if parts == "q" else 2
+    i_i = lax.broadcasted_iota(jnp.int32, (n_parts * per_group, n_parts * hd), 0)
+    n_i = lax.broadcasted_iota(jnp.int32, (n_parts * per_group, n_parts * hd), 1)
     place = [
         (n_i == (i_i // per_group) * hd + g * per_group + i_i % per_group).astype(bf16)
         for g in range(gph)
@@ -64,15 +68,17 @@
                 pieces = []
                 for e in range(pair):
                     g = m * pair + e
-                    w = wd_ref[k * gph + g, pl.ds(t * width, width), :]
+                    w = wd_ref[k * gph + g, pl.ds(t * width, width), pl.ds(first_part * per_group, n_parts * per_group)]
                     pieces.append(jnp.dot(w, place[g], preferred_element_type=f32).astype(bf16))
                 wp = jnp.concatenate(pieces, axis=0)
                 col = (k * gph + m * pair) * width
                 part = jnp.dot(picked[t][:, col : col + 128], wp, preferred_element_type=f32)
                 acc = part if acc is None else acc + part
-        q_ref[k] = normalize(acc[:, :hd]).astype(bf16)
-        kv_ref[0, 0, k] = normalize(acc[:, hd : 2 * hd]).astype(bf16)
-        kv_ref[1, 0, k] = acc[:, 2 * hd :].astype(bf16)
+        if parts == "q":
+            outs[0][k] = normalize(acc[:, :hd]).astype(bf16)
+        else:
+            outs[0][0, 0, k] = normalize(acc[:, :hd]).astype(bf16)
+            outs[0][1, 0, k] = acc[:, hd:].astype(bf16)
 
 
 def post_kernel(idx_ref, sharp_ref, q_ref, kv_ref, wup_ref, res_ref, oct_ref, out_ref, att_scr):
@@ -145,17 +151,22 @@
     left_rim = shifted_2(residual_stream[byte_rows - rim_rows :], "seq", 1)
     vmem = pl.BlockSpec(memory_space=pltpu.VMEM)
     smem = pl.BlockSpec(memory_space=pltpu.SMEM)
-    queries, stacked = pl.pallas_call(
-        shorten_kernel,
-        out_shape=(
-            jax.ShapeDtypeStruct((attention_number, tokens_here, head_size), jnp.bfloat16),
-            jax.ShapeDtypeStruct((2, 1, attention_number, tokens_here, head_size), jnp.bfloat16),
-        ),
+    params = pltpu.CompilerParams(vmem_limit_bytes=60 * 1024 * 1024)
+    stacked = pl.pallas_call(
+        functools.partial(shorten_kernel, parts="kv"),
+        out_shape=jax.ShapeDtypeStruct((2, 1, attention_number, tokens_here, head_size), jnp.bfloat16),
         in_specs=[vmem, vmem, vmem],
-        out_specs=(vmem, vmem),
-        compiler_params=pltpu.CompilerParams(vmem_limit_bytes=60 * 1024 * 1024),
+        out_specs=vmem,
+        compiler_params=params,
     )(residual_stream, left_rim, downsampling_filter)
     gathered = lax.all_gather(stacked, "seq", axis=1, tiled=True)
+    queries = pl.pallas_call(
+        functools.partial(shorten_kernel, parts="q"),
+        out_shape=jax.ShapeDtypeStruct((attention_number, tokens_here, head_size), jnp.bfloat16),
+        in_specs=[vmem, vmem, vmem],
+        out_specs=vmem,
+        compiler_params=params,
+    )(residual_stream, left_rim, downsampling_filter)
     my_index = lax.axis_index("seq").astype(jnp.int32).reshape(1)
     wup = widening_blocks(widening_filter, attention_number)
     return pl.pallas_call(

time: 118 us -> 109 us (0.924)
  waiting for transfers between devices: 52.4 us -> 46.7 us
  Pallas kernels: 30.3 us -> 27.3 us
    all_gather x1, waiting for transfers between devices: 52.4 us -> 46.7 us  [on_device(): gathered = lax.all_gather(stacked, 'seq', axis=1, tiled=True)]
    pallas_call x1 -> x2, Pallas kernels: 15.5 us -> 12.5 us  [the longest x1 6.79 us: on_device(): pl.pallas_call(functools.partial(shorten_kernel, parts='kv'), out_shape=j...]
  transfers between devices with their start and end apart: 2 -> 2, of which waited for: 1 -> 1; matrix products, arithmetic and copies ran while one was open for 14% -> 16% of each run, Pallas kernels for 0% -> 5%
where the time goes in v6:
time: 109 us; the launch traced here: 107 us
  waiting for transfers between devices  46.7 us (43%)
  Pallas kernels  27.3 us (25%)
  local copies, waits for them, and re-layouts  16.7 us (15%)
  between operations  13.5 us (12%)
  starting transfers between devices  1.74 us (2%)
  other arithmetic  1.51 us (1%)
    all_gather x1, waiting for transfers between devices, on_device(): gathered = lax.all_gather(stacked, 'seq', axis=1, tiled=True)  46.7 us
    pallas_call x1, Pallas kernels, on_device(): pl.pallas_call(post_kernel, out_shape=jax.ShapeDtypeStruct((byte_rows, oc...  14.8 us
    broadcast_in_dim x4, local copies, waits for them, and re-layouts, widening_blocks(): blocks = jnp.where(eye, wf, jnp.zeros((), wf.dtype))  10.8 us
    pallas_call x1, Pallas kernels, on_device(): pl.pallas_call(functools.partial(shorten_kernel, parts='kv'), out_shape=j...  6.79 us
    pallas_call x1, Pallas kernels, on_device(): pl.pallas_call(functools.partial(shorten_kernel, parts='q'), out_shape=ja...  5.69 us
    unnamed x5, local copies, waits for them, and re-layouts  4.44 us
  transfers between devices with their start and end apart: 2, of which 1 were waited for; matrix products, arithmetic and copies ran while one was open for 16% of the time, Pallas kernels for 5%

profile of v6, /device:TPU:6, one launch (start us, length us, event | category | flops | bytes accessed | tf_op | source)
XLA Modules:
  0.0 107.4 jit_solution(10179648705178284922)
XLA Ops:
  6.5 0.0 all-gather.2.cloned.1.call-start
  6.5 0.8 slice.3
  7.3 1.7 %collective-permute-start = (bf16[3,2048]{1,0:T(4,128)(2,1)S(1)}, bf16[3,2048]{1,0:T(4,128)(2,1)S(1)}, u32[]{:S(2)}, u32[]{:S(2)}) collective-permute-start(bf16[3,2048]{1,0:T(4,128)(2,1)S(1)} %slice.3), channel_id=1, source_target_pairs={{0,1},{1,2},{2,3},{3,4},{4,5},{5,6},{6,7},{7,8},{8,9},{9,10},{10,1... | collective-permute-start | bytes 36872 | tf_op jit(solution)/shard_map/ppermute | solution.py:16
  9.1 3.8 %copy.6.wd_ref = bf16[32,256,96]{2,1,0:T(8,128)(2,1)} copy(bf16[32,256,96]{1,2,0:T(8,128)(2,1)} %param.7) | data formatting | bytes 3145728 | tf_op args[2]
  12.9 0.0 copy-start
  12.9 0.0 collective-permute-done.rim_ref
  12.9 0.0 copy-start.1
  12.9 0.6 copy-done.1
  13.5 6.8 %shard_map.56 = bf16[2,1,8,128,128]{4,3,2,1,0:T(8,128)(2,1)} custom-call(bf16[512,2048]{1,0:T(8,128)(2,1)} %res_ref.5, bf16[3,2048]{1,0:T(4,128)(2,1)} %copy-done.1, bf16[32,256,96]{2,1,0:T(8,128)(2,1)} %copy.6.wd_ref), custom_call_target="tpu_custom_call" | custom-call | tf_op jit(solution)/shard_map/pallas_call | solution.py:155
  20.3 0.0 all-gather.2.cloned.1.call-update
  20.3 0.0 copy-done
  20.3 0.4 reshape.11
  20.7 0.2 copy.8
  21.0 4.4 %broadcast_in_dim.31 = bf16[4,8,4,32,4,64]{5,4,3,2,1,0:T(4,128)(2,1)} broadcast(bf16[4,8,4,32,64]{4,3,2,1,0:T(8,128)(2,1)S(1)} %copy.8), dimensions={0,1,2,3,5} | broadcast | bytes 2621440 | tf_op jit(solution)/shard_map/jit(_where)/broadcast_in_dim | solution.py:30
  25.4 6.1 %broadcast_in_dim.32 = bf16[4,8,128,256]{3,2,1,0:T(8,128)(2,1)S(1)} reshape(bf16[4,8,4,32,4,64]{5,4,3,2,1,0:T(4,128)(2,1)} %broadcast_in_dim.31) | data formatting | bytes 4194304 | tf_op jit(solution)/shard_map/jit(_where)/broadcast_in_dim | solution.py:30
  31.6 0.1 broadcast_in_dim.28
  31.7 0.2 broadcast_in_dim.29
  31.8 1.5 %broadcast_select_fusion.wup_ref = bf16[4,8,128,256]{3,2,1,0:T(8,128)(2,1)} fusion(bf16[4,8,128,256]{3,2,1,0:T(8,128)(2,1)S(1)} %broadcast_in_dim.32, pred[128,256]{1,0:T(8,128)(4,1)S(1)} %broadcast_in_dim.29), kind=kLoop, calls=%fused_computation | loop fusion | flops 1048576 | bytes 4227072 | tf_op jit(solution)/shard_map/jit(_where)/select_n | solution.py:30
  33.3 5.7 %shard_map.55.q_ref = bf16[8,128,128]{2,1,0:T(8,128)(2,1)} custom-call(bf16[512,2048]{1,0:T(8,128)(2,1)} %res_ref.5, bf16[3,2048]{1,0:T(4,128)(2,1)} %copy-done.1, bf16[32,256,96]{2,1,0:T(8,128)(2,1)} %copy.6.wd_ref), custom_call_target="tpu_custom_call" | custom-call | tf_op jit(solution)/shard_map/pallas_call | solution.py:163
  39.0 46.7 %all-gather.2.cloned.1.call-done.kv_ref = bf16[2,16,8,128,128]{4,3,2,1,0:T(8,128)(2,1)} async-done(((bf16[2,1,8,128,128]{4,3,2,1,0:T(8,128)(2,1)}), bf16[2,16,8,128,128]{4,3,2,1,0:T(8,128)(2,1)}) %all-gather.2.cloned.1.call-update) | async-done | bytes 8388624 | tf_op jit(solution)/shard_map/all_gather | solution.py:162
  85.7 14.8 %shard_map.57 = bf16[512,256]{1,0:T(8,128)(2,1)} custom-call(s32[1]{0:T(128)} %bitcast.idx_ref, f32[8]{0:T(128)} %sharp_ref.1, bf16[8,128,128]{2,1,0:T(8,128)(2,1)} %shard_map.55.q_ref, bf16[2,16,8,128,128]{4,3,2,1,0:T(8,128)(2,1)} %all-gather.2.cloned.1.call-done.kv_ref, bf16[4,8,128,256]{3,2,1,0:T(8,128)(2,1)} %broadcast_select_fusion.wup_ref, ...), custom_call_target="tpu_custom_call" | custom-call | tf_op jit(solution)/shard_map/pallas_call | solution.py:172
  (1 shorter events, 0.0 us)
Async XLA Ops:
  6.5 79.2 %all-gather.2.cloned.1.call-start = ((), (), s32[]{:S(2)}) async-start(), calls=%async_computation | async-start | bytes 8912896 | tf_op jit(solution)/shard_map/all_gather | solution.py:162
  7.3 5.6 %collective-permute-start = (bf16[3,2048]{1,0:T(4,128)(2,1)S(1)}, bf16[3,2048]{1,0:T(4,128)(2,1)S(1)}, u32[]{:S(2)}, u32[]{:S(2)}) collective-permute-start(bf16[3,2048]{1,0:T(4,128)(2,1)S(1)} %slice.3), channel_id=1, source_target_pairs={{0,1},{1,2},{2,3},{3,4},{4,5},{5,6},{6,7},{7,8},{8,9},{9,10},{10,1... | collective-permute-start | bytes 36872 | tf_op jit(solution)/shard_map/ppermute | solution.py:16
  12.9 7.4 %copy-start = (bf16[32,32,256]{2,1,0:T(8,128)(2,1)S(1)}, bf16[32,32,256]{2,1,0:T(8,128)(2,1)}, u32[]{:S(2)}) copy-start(bf16[32,32,256]{2,1,0:T(8,128)(2,1)} %param.9) | copy-start | bytes 1572868
  12.9 0.6 copy-start.1
Sparse Core Ops, SparseCore 0:
  20.4 65.2 all-gather.1

commit v7 on v6

--- a/solution.py
+++ b/solution.py
@@ -77,7 +77,7 @@
         if parts == "q":
             outs[0][k] = normalize(acc[:, :hd]).astype(bf16)
         else:
-            outs[0][0, 0, k] = normalize(acc[:, :hd]).astype(bf16)
+            outs[0][0, 0, k] = normalize(acc[:, :hd]).T.astype(bf16)
             outs[0][1, 0, k] = acc[:, hd:].astype(bf16)
 
 
@@ -92,9 +92,9 @@
     for h in range(heads):
         q = q_ref[h]
         sharp = sharp_ref[h]
-        keys = jnp.concatenate([kv_ref[0, d, h] for d in range(nb)], axis=0)
+        keys_t = jnp.concatenate([kv_ref[0, d, h] for d in range(nb)], axis=1)
         vals = jnp.concatenate([kv_ref[1, d, h] for d in range(nb)], axis=0)
-        s = lax.dot_general(q, keys, (((1,), (1,)), ((), ())), preferred_element_type=f32) * sharp
+        s = jnp.dot(q, keys_t, preferred_element_type=f32) * sharp
         w = jnp.where(visible, jnp.exp(s - sharp), jnp.zeros((), f32))
         den = jnp.sum(w, axis=1, keepdims=True)
         num = jnp.dot(w.astype(bf16), vals, preferred_element_type=f32)
@@ -128,10 +128,9 @@
         scale = lax.rsqrt(ss / width + 1e-05)
         acc = None
         for k in range(n_chunks):
-            part = lax.dot_general(
+            part = jnp.dot(
                 (hid[k] * scale).astype(bf16),
-                oct_ref[:, pl.ds(k * cout, cout)],
-                (((1,), (1,)), ((), ())),
+                oct_ref[pl.ds(k * cout, cout), :],
                 preferred_element_type=f32,
             )
             acc = part if acc is None else acc + part
@@ -176,7 +175,7 @@
         out_specs=vmem,
         scratch_shapes=[pltpu.VMEM((tokens_here, attention_number * head_size), jnp.bfloat16)],
         compiler_params=pltpu.CompilerParams(vmem_limit_bytes=60 * 1024 * 1024),
-    )(my_index, sharpness_factor, queries, gathered, wup, residual_stream, octet_readout)
+    )(my_index, sharpness_factor, queries, gathered, wup, residual_stream, octet_readout.T)
 
 
 def solution(mesh):

time: 109 us -> 108 us (level)
  Pallas kernels: 27.3 us -> 26 us
  waiting for transfers between devices: 46.7 us -> 45.5 us
  local copies, waits for them, and re-layouts: 16.7 us -> 17.9 us
    pallas_call x1, Pallas kernels: 14.8 us -> 13.5 us  [on_device(): pl.pallas_call(post_kernel, out_shape=jax.ShapeDtypeStruct((byte_rows, oc...]
    unnamed x5 -> x8, local copies, waits for them, and re-layouts: 4.44 us -> 5.75 us
    all_gather x1, waiting for transfers between devices: 46.7 us -> 45.5 us  [on_device(): gathered = lax.all_gather(stacked, 'seq', axis=1, tiled=True)]
  transfers between devices with their start and end apart: 2 -> 2, of which waited for: 1 -> 1; matrix products, arithmetic and copies ran while one was open for 16% -> 17% of each run, Pallas kernels for 5% -> 5%
where the time goes in v7:
time: 108 us; the launch traced here: 106 us
  waiting for transfers between devices  45.5 us (42%)
  Pallas kernels  26 us (24%)
  local copies, waits for them, and re-layouts  17.9 us (17%)
  between operations  13.5 us (12%)
  starting transfers between devices  1.74 us (2%)
  other arithmetic  1.5 us (1%)
    all_gather x1, waiting for transfers between devices, on_device(): gathered = lax.all_gather(stacked, 'seq', axis=1, tiled=True)  45.5 us
    pallas_call x1, Pallas kernels, on_device(): pl.pallas_call(post_kernel, out_shape=jax.ShapeDtypeStruct((byte_rows, oc...  13.5 us
    broadcast_in_dim x4, local copies, waits for them, and re-layouts, widening_blocks(): blocks = jnp.where(eye, wf, jnp.zeros((), wf.dtype))  10.7 us
    pallas_call x1, Pallas kernels, on_device(): pl.pallas_call(functools.partial(shorten_kernel, parts='kv'), out_shape=j...  6.85 us
    unnamed x8, local copies, waits for them, and re-layouts  5.75 us
    pallas_call x1, Pallas kernels, on_device(): pl.pallas_call(functools.partial(shorten_kernel, parts='q'), out_shape=ja...  5.71 us
  transfers between devices with their start and end apart: 2, of which 1 were waited for; matrix products, arithmetic and copies ran while one was open for 17% of the time, Pallas kernels for 5%

profile of v7, /device:TPU:6, one launch (start us, length us, event | category | flops | bytes accessed | tf_op | source)
XLA Modules:
  0.0 106.1 jit_solution(6915940876597908187)
XLA Ops:
  6.5 0.0 all-gather.2.cloned.1.call-start
  6.5 0.8 slice.3
  7.3 1.7 %collective-permute-start = (bf16[3,2048]{1,0:T(4,128)(2,1)S(1)}, bf16[3,2048]{1,0:T(4,128)(2,1)S(1)}, u32[]{:S(2)}, u32[]{:S(2)}) collective-permute-start(bf16[3,2048]{1,0:T(4,128)(2,1)S(1)} %slice.3), channel_id=1, source_target_pairs={{0,1},{1,2},{2,3},{3,4},{4,5},{5,6},{6,7},{7,8},{8,9},{9,10},{10,1... | collective-permute-start | bytes 36872 | tf_op jit(solution)/shard_map/ppermute | solution.py:16
  9.1 3.8 %copy.6.wd_ref = bf16[32,256,96]{2,1,0:T(8,128)(2,1)} copy(bf16[32,256,96]{1,2,0:T(8,128)(2,1)} %param.7) | data formatting | bytes 3145728 | tf_op args[2]
  12.9 0.0 copy-start.1
  12.9 0.0 collective-permute-done.rim_ref
  12.9 0.0 copy-start.2
  12.9 0.6 copy-done.2
  13.5 6.8 %shard_map.56 = bf16[2,1,8,128,128]{4,3,2,1,0:T(8,128)(2,1)} custom-call(bf16[512,2048]{1,0:T(8,128)(2,1)} %res_ref.5, bf16[3,2048]{1,0:T(4,128)(2,1)} %copy-done.2, bf16[32,256,96]{2,1,0:T(8,128)(2,1)} %copy.6.wd_ref), custom_call_target="tpu_custom_call" | custom-call | tf_op jit(solution)/shard_map/pallas_call | solution.py:154
  20.4 0.0 all-gather.2.cloned.1.call-update
  20.4 0.0 copy-done.1
  20.4 0.4 reshape.11
  20.8 0.2 copy.8
  21.1 4.4 %broadcast_in_dim.31 = bf16[4,8,4,32,4,64]{5,4,3,2,1,0:T(4,128)(2,1)} broadcast(bf16[4,8,4,32,64]{4,3,2,1,0:T(8,128)(2,1)S(1)} %copy.8), dimensions={0,1,2,3,5} | broadcast | bytes 2621440 | tf_op jit(solution)/shard_map/jit(_where)/broadcast_in_dim | solution.py:30
  25.5 0.0 copy-start
  25.5 6.0 %broadcast_in_dim.32 = bf16[4,8,128,256]{3,2,1,0:T(8,128)(2,1)S(1)} reshape(bf16[4,8,4,32,4,64]{5,4,3,2,1,0:T(4,128)(2,1)} %broadcast_in_dim.31) | data formatting | bytes 4194304 | tf_op jit(solution)/shard_map/jit(_where)/broadcast_in_dim | solution.py:30
  31.5 0.1 broadcast_in_dim.28
  31.6 0.2 broadcast_in_dim.29
  31.8 0.0 copy-done
  31.8 1.3 %copy.9 = bf16[256,2048]{0,1:T(8,128)(2,1)} copy(bf16[256,2048]{1,0:T(8,128)(2,1)S(1)} %copy-done) | data formatting | bytes 2097152 | tf_op args[1]
  33.1 1.5 %broadcast_select_fusion.wup_ref = bf16[4,8,128,256]{3,2,1,0:T(8,128)(2,1)} fusion(bf16[4,8,128,256]{3,2,1,0:T(8,128)(2,1)S(1)} %broadcast_in_dim.32, pred[128,256]{1,0:T(8,128)(4,1)S(1)} %broadcast_in_dim.29), kind=kLoop, calls=%fused_computation | loop fusion | flops 1048576 | bytes 4227072 | tf_op jit(solution)/shard_map/jit(_where)/select_n | solution.py:30
  34.6 5.7 %shard_map.55.q_ref = bf16[8,128,128]{2,1,0:T(8,128)(2,1)} custom-call(bf16[512,2048]{1,0:T(8,128)(2,1)} %res_ref.5, bf16[3,2048]{1,0:T(4,128)(2,1)} %copy-done.2, bf16[32,256,96]{2,1,0:T(8,128)(2,1)} %copy.6.wd_ref), custom_call_target="tpu_custom_call" | custom-call | tf_op jit(solution)/shard_map/pallas_call | solution.py:162
  40.3 45.5 %all-gather.2.cloned.1.call-done.kv_ref = bf16[2,16,8,128,128]{4,3,2,1,0:T(8,128)(2,1)} async-done(((bf16[2,1,8,128,128]{4,3,2,1,0:T(8,128)(2,1)}), bf16[2,16,8,128,128]{4,3,2,1,0:T(8,128)(2,1)}) %all-gather.2.cloned.1.call-update) | async-done | bytes 8388624 | tf_op jit(solution)/shard_map/all_gather | solution.py:161
  85.8 13.5 %shard_map.57 = bf16[512,256]{1,0:T(8,128)(2,1)} custom-call(s32[1]{0:T(128)} %bitcast.idx_ref, f32[8]{0:T(128)} %sharp_ref.1, bf16[8,128,128]{2,1,0:T(8,128)(2,1)} %shard_map.55.q_ref, bf16[2,16,8,128,128]{4,3,2,1,0:T(8,128)(2,1)} %all-gather.2.cloned.1.call-done.kv_ref, bf16[4,8,128,256]{3,2,1,0:T(8,128)(2,1)} %broadcast_select_fusion.wup_ref, ...), custom_call_target="tpu_custom_call" | custom-call | tf_op jit(solution)/shard_map/pallas_call | solution.py:171
  (1 shorter events, 0.0 us)
Async XLA Ops:
  6.5 79.3 %all-gather.2.cloned.1.call-start = ((), (), s32[]{:S(2)}) async-start(), calls=%async_computation | async-start | bytes 8912896 | tf_op jit(solution)/shard_map/all_gather | solution.py:161
  7.3 5.6 %collective-permute-start = (bf16[3,2048]{1,0:T(4,128)(2,1)S(1)}, bf16[3,2048]{1,0:T(4,128)(2,1)S(1)}, u32[]{:S(2)}, u32[]{:S(2)}) collective-permute-start(bf16[3,2048]{1,0:T(4,128)(2,1)S(1)} %slice.3), channel_id=1, source_target_pairs={{0,1},{1,2},{2,3},{3,4},{4,5},{5,6},{6,7},{7,8},{8,9},{9,10},{10,1... | collective-permute-start | bytes 36872 | tf_op jit(solution)/shard_map/ppermute | solution.py:16
  12.9 7.5 %copy-start.1 = (bf16[32,32,256]{2,1,0:T(8,128)(2,1)S(1)}, bf16[32,32,256]{2,1,0:T(8,128)(2,1)}, u32[]{:S(2)}) copy-start(bf16[32,32,256]{2,1,0:T(8,128)(2,1)} %param.9) | copy-start | bytes 1572868
  12.9 0.6 copy-start.2
  25.5 6.3 %copy-start = (bf16[256,2048]{1,0:T(8,128)(2,1)S(1)}, bf16[256,2048]{1,0:T(8,128)(2,1)}, u32[]{:S(2)}) copy-start(bf16[256,2048]{1,0:T(8,128)(2,1)} %param.6) | copy-start | bytes 3145732
Sparse Core Ops, SparseCore 0:
  20.5 65.2 all-gather.1

commit v8 on v7

--- a/solution.py
+++ b/solution.py
@@ -37,7 +37,7 @@
     tokens = rows // SHORTEN
     heads = outs[0].shape[-3]
     hd = outs[0].shape[-1]
-    groups, span, channels = wd_ref.shape
+    groups, channels, span = wd_ref.shape
     gph = groups // heads
     width = span // SHORTEN
     per_group = channels // 3
@@ -68,8 +68,10 @@
                 pieces = []
                 for e in range(pair):
                     g = m * pair + e
-                    w = wd_ref[k * gph + g, pl.ds(t * width, width), pl.ds(first_part * per_group, n_parts * per_group)]
-                    pieces.append(jnp.dot(w, place[g], preferred_element_type=f32).astype(bf16))
+                    w = wd_ref[k * gph + g, pl.ds(first_part * per_group, n_parts * per_group), pl.ds(t * width, width)]
+                    pieces.append(lax.dot_general(
+                        w, place[g], (((0,), (0,)), ((), ())), preferred_element_type=f32
+                    ).astype(bf16))
                 wp = jnp.concatenate(pieces, axis=0)
                 col = (k * gph + m * pair) * width
                 part = jnp.dot(picked[t][:, col : col + 128], wp, preferred_element_type=f32)
@@ -151,13 +153,14 @@
     vmem = pl.BlockSpec(memory_space=pltpu.VMEM)
     smem = pl.BlockSpec(memory_space=pltpu.SMEM)
     params = pltpu.CompilerParams(vmem_limit_bytes=60 * 1024 * 1024)
+    filter_t = jnp.swapaxes(downsampling_filter, 1, 2)
     stacked = pl.pallas_call(
         functools.partial(shorten_kernel, parts="kv"),
         out_shape=jax.ShapeDtypeStruct((2, 1, attention_number, tokens_here, head_size), jnp.bfloat16),
         in_specs=[vmem, vmem, vmem],
         out_specs=vmem,
         compiler_params=params,
-    )(residual_stream, left_rim, downsampling_filter)
+    )(residual_stream, left_rim, filter_t)
     gathered = lax.all_gather(stacked, "seq", axis=1, tiled=True)
     queries = pl.pallas_call(
         functools.partial(shorten_kernel, parts="q"),
@@ -165,7 +168,7 @@
         in_specs=[vmem, vmem, vmem],
         out_specs=vmem,
         compiler_params=params,
-    )(residual_stream, left_rim, downsampling_filter)
+    )(residual_stream, left_rim, filter_t)
     my_index = lax.axis_index("seq").astype(jnp.int32).reshape(1)
     wup = widening_blocks(widening_filter, attention_number)
     return pl.pallas_call(

time: 108 us -> 107 us (level)
  local copies, waits for them, and re-layouts: 17.9 us -> 14.1 us
  waiting for transfers between devices: 45.5 us -> 48.7 us
    unnamed x8 -> x7, local copies, waits for them, and re-layouts: 5.75 us -> 1.92 us
    all_gather x1, waiting for transfers between devices: 45.5 us -> 47.9 us  [on_device(): gathered = lax.all_gather(stacked, 'seq', axis=1, tiled=True)]
  transfers between devices with their start and end apart: 2 -> 2, of which waited for: 1 -> 2; matrix products, arithmetic and copies ran while one was open for 17% -> 13% of each run, Pallas kernels for 5% -> 5%
where the time goes in v8:
time: 107 us; the launch traced here: 105 us
  waiting for transfers between devices  48.7 us (46%)
  Pallas kernels  25.8 us (24%)
  local copies, waits for them, and re-layouts  14.1 us (13%)
  between operations  13.5 us (13%)
  starting transfers between devices  1.74 us (2%)
  other arithmetic  1.5 us (1%)
    all_gather x1, waiting for transfers between devices, on_device(): gathered = lax.all_gather(stacked, 'seq', axis=1, tiled=True)  47.9 us
    pallas_call x1, Pallas kernels, on_device(): pl.pallas_call(post_kernel, out_shape=jax.ShapeDtypeStruct((byte_rows, oc...  13.5 us
    broadcast_in_dim x4, local copies, waits for them, and re-layouts, widening_blocks(): blocks = jnp.where(eye, wf, jnp.zeros((), wf.dtype))  10.7 us
    pallas_call x1, Pallas kernels, on_device(): pl.pallas_call(functools.partial(shorten_kernel, parts='kv'), out_shape=j...  6.77 us
    pallas_call x1, Pallas kernels, on_device(): pl.pallas_call(functools.partial(shorten_kernel, parts='q'), out_shape=ja...  5.56 us
  transfers between devices with their start and end apart: 2, of which 2 were waited for; matrix products, arithmetic and copies ran while one was open for 13% of the time, Pallas kernels for 5%

profile of v8, /device:TPU:6, one launch (start us, length us, event | category | flops | bytes accessed | tf_op | source)
XLA Modules:
  0.0 105.3 jit_solution(1945321746266343891)
XLA Ops:
  6.5 0.0 all-gather.2.cloned.1.call-start
  6.5 0.8 slice.3
  7.3 1.7 %collective-permute-start = (bf16[3,2048]{1,0:T(4,128)(2,1)S(1)}, bf16[3,2048]{1,0:T(4,128)(2,1)S(1)}, u32[]{:S(2)}, u32[]{:S(2)}) collective-permute-start(bf16[3,2048]{1,0:T(4,128)(2,1)S(1)} %slice.3), channel_id=1, source_target_pairs={{0,1},{1,2},{2,3},{3,4},{4,5},{5,6},{6,7},{7,8},{8,9},{9,10},{10,1... | collective-permute-start | bytes 36872 | tf_op jit(solution)/shard_map/ppermute | solution.py:16
  9.1 0.8 collective-permute-done.rim_ref
  9.9 0.0 copy-start.2
  9.9 0.6 copy-done.2
  10.5 0.0 copy-start.1
  10.5 6.8 %shard_map.56 = bf16[2,1,8,128,128]{4,3,2,1,0:T(8,128)(2,1)} custom-call(bf16[512,2048]{1,0:T(8,128)(2,1)} %res_ref.5, bf16[3,2048]{1,0:T(4,128)(2,1)} %copy-done.2, bf16[32,96,256]{2,1,0:T(8,128)(2,1)} %bitcast.4), custom_call_target="tpu_custom_call" | custom-call | tf_op jit(solution)/shard_map/pallas_call | solution.py:157
  17.3 0.0 all-gather.2.cloned.1.call-update
  17.3 0.0 copy-done.1
  17.3 0.4 reshape.11
  17.7 0.2 copy.6
  17.9 4.4 %broadcast_in_dim.31 = bf16[4,8,4,32,4,64]{5,4,3,2,1,0:T(4,128)(2,1)} broadcast(bf16[4,8,4,32,64]{4,3,2,1,0:T(8,128)(2,1)S(1)} %copy.6), dimensions={0,1,2,3,5} | broadcast | bytes 2621440 | tf_op jit(solution)/shard_map/jit(_where)/broadcast_in_dim | solution.py:30
  22.4 0.0 copy-start
  22.4 6.0 %broadcast_in_dim.32 = bf16[4,8,128,256]{3,2,1,0:T(8,128)(2,1)S(1)} reshape(bf16[4,8,4,32,4,64]{5,4,3,2,1,0:T(4,128)(2,1)} %broadcast_in_dim.31) | data formatting | bytes 4194304 | tf_op jit(solution)/shard_map/jit(_where)/broadcast_in_dim | solution.py:30
  28.4 0.1 broadcast_in_dim.28
  28.5 0.2 broadcast_in_dim.29
  28.7 0.0 copy-done
  28.7 1.3 %copy.7 = bf16[256,2048]{0,1:T(8,128)(2,1)} copy(bf16[256,2048]{1,0:T(8,128)(2,1)S(1)} %copy-done) | data formatting | bytes 2097152 | tf_op args[1]
  30.0 1.5 %broadcast_select_fusion.wup_ref = bf16[4,8,128,256]{3,2,1,0:T(8,128)(2,1)} fusion(bf16[4,8,128,256]{3,2,1,0:T(8,128)(2,1)S(1)} %broadcast_in_dim.32, pred[128,256]{1,0:T(8,128)(4,1)S(1)} %broadcast_in_dim.29), kind=kLoop, calls=%fused_computation | loop fusion | flops 1048576 | bytes 4227072 | tf_op jit(solution)/shard_map/jit(_where)/select_n | solution.py:30
  31.5 5.6 %shard_map.55.q_ref = bf16[8,128,128]{2,1,0:T(8,128)(2,1)} custom-call(bf16[512,2048]{1,0:T(8,128)(2,1)} %res_ref.5, bf16[3,2048]{1,0:T(4,128)(2,1)} %copy-done.2, bf16[32,96,256]{2,1,0:T(8,128)(2,1)} %bitcast.5), custom_call_target="tpu_custom_call" | custom-call | tf_op jit(solution)/shard_map/pallas_call | solution.py:165
  37.1 47.9 %all-gather.2.cloned.1.call-done.kv_ref = bf16[2,16,8,128,128]{4,3,2,1,0:T(8,128)(2,1)} async-done(((bf16[2,1,8,128,128]{4,3,2,1,0:T(8,128)(2,1)}), bf16[2,16,8,128,128]{4,3,2,1,0:T(8,128)(2,1)}) %all-gather.2.cloned.1.call-update) | async-done | bytes 8388624 | tf_op jit(solution)/shard_map/all_gather | solution.py:164
  85.0 13.5 %shard_map.57 = bf16[512,256]{1,0:T(8,128)(2,1)} custom-call(s32[1]{0:T(128)} %bitcast.idx_ref, f32[8]{0:T(128)} %sharp_ref.1, bf16[8,128,128]{2,1,0:T(8,128)(2,1)} %shard_map.55.q_ref, bf16[2,16,8,128,128]{4,3,2,1,0:T(8,128)(2,1)} %all-gather.2.cloned.1.call-done.kv_ref, bf16[4,8,128,256]{3,2,1,0:T(8,128)(2,1)} %broadcast_select_fusion.wup_ref, ...), custom_call_target="tpu_custom_call" | custom-call | tf_op jit(solution)/shard_map/pallas_call | solution.py:174
  (1 shorter events, 0.0 us)
Async XLA Ops:
  6.5 78.4 %all-gather.2.cloned.1.call-start = ((), (), s32[]{:S(2)}) async-start(), calls=%async_computation | async-start | bytes 8912896 | tf_op jit(solution)/shard_map/all_gather | solution.py:164
  7.3 2.6 %collective-permute-start = (bf16[3,2048]{1,0:T(4,128)(2,1)S(1)}, bf16[3,2048]{1,0:T(4,128)(2,1)S(1)}, u32[]{:S(2)}, u32[]{:S(2)}) collective-permute-start(bf16[3,2048]{1,0:T(4,128)(2,1)S(1)} %slice.3), channel_id=1, source_target_pairs={{0,1},{1,2},{2,3},{3,4},{4,5},{5,6},{6,7},{7,8},{8,9},{9,10},{10,1... | collective-permute-start | bytes 36872 | tf_op jit(solution)/shard_map/ppermute | solution.py:16
  9.9 0.6 copy-start.2
  10.5 6.8 %copy-start.1 = (bf16[32,32,256]{2,1,0:T(8,128)(2,1)S(1)}, bf16[32,32,256]{2,1,0:T(8,128)(2,1)}, u32[]{:S(2)}) copy-start(bf16[32,32,256]{2,1,0:T(8,128)(2,1)} %param.9) | copy-start | bytes 1572868
  22.4 6.3 %copy-start = (bf16[256,2048]{1,0:T(8,128)(2,1)S(1)}, bf16[256,2048]{1,0:T(8,128)(2,1)}, u32[]{:S(2)}) copy-start(bf16[256,2048]{1,0:T(8,128)(2,1)} %param.6) | copy-start | bytes 3145732
Sparse Core Ops, SparseCore 0:
  17.4 67.5 all-gather.1

commit v9 on v8

--- a/solution.py
+++ b/solution.py
@@ -28,7 +28,8 @@
     wf = wf.transpose(3, 0, 1, 2, 4)[:, :, :, :, None, :]
     eye = jnp.eye(gph, dtype=jnp.bool_)[:, None, :, None]
     blocks = jnp.where(eye, wf, jnp.zeros((), wf.dtype))
-    return blocks.reshape(SHORTEN, heads, gph * per_group, gph * width)
+    blocks = blocks.reshape(SHORTEN, heads, gph * per_group, gph * width).transpose(1, 0, 2, 3)
+    return blocks.reshape(heads, SHORTEN * gph * per_group, gph * width)
 
 
 def shorten_kernel(res_ref, rim_ref, wd_ref, *outs, parts):
@@ -105,9 +106,9 @@
     rows, width = res_ref.shape
     row_blocks = rows // 128
     tok_blk = 128 // SHORTEN
-    n_chunks = wup_ref.shape[1]
-    cin = wup_ref.shape[2]
-    cout = wup_ref.shape[3]
+    n_chunks = wup_ref.shape[0]
+    cin = wup_ref.shape[1] // SHORTEN
+    cout = wup_ref.shape[2]
     r_i = lax.broadcasted_iota(jnp.int32, (128, tok_blk), 0)
     j_i = lax.broadcasted_iota(jnp.int32, (128, tok_blk), 1)
     for rb in range(row_blocks):
@@ -119,11 +120,8 @@
         hid = []
         ss = jnp.zeros((128, 1), f32)
         for k in range(n_chunks):
-            u = jnp.dot(expanded[0][:, k * cin : (k + 1) * cin], wup_ref[0, k], preferred_element_type=f32)
-            for t in range(1, SHORTEN):
-                u = u + jnp.dot(
-                    expanded[t][:, k * cin : (k + 1) * cin], wup_ref[t, k], preferred_element_type=f32
-                )
+            lhs = jnp.concatenate([expanded[t][:, k * cin : (k + 1) * cin] for t in range(SHORTEN)], axis=1)
+            u = jnp.dot(lhs, wup_ref[k], preferred_element_type=f32)
             hcol = res_ref[pl.ds(rb * 128, 128), pl.ds(k * cout, cout)].astype(f32) + u
             hid.append(hcol)
             ss = ss + jnp.sum(hcol * hcol, axis=1, keepdims=True)

time: 107 us -> 106 us (level)
  transfers between devices with their start and end apart: 2 -> 2, of which waited for: 2 -> 2; matrix products, arithmetic and copies ran while one was open for 13% -> 14% of each run, Pallas kernels for 5% -> 5%
where the time goes in v9:
time: 106 us; the launch traced here: 104 us
  waiting for transfers between devices  48.7 us (46%)
  Pallas kernels  24.8 us (23%)
  local copies, waits for them, and re-layouts  14.1 us (13%)
  between operations  13.5 us (13%)
  starting transfers between devices  1.74 us (2%)
  other arithmetic  1.5 us (1%)
    all_gather x1, waiting for transfers between devices, on_device(): gathered = lax.all_gather(stacked, 'seq', axis=1, tiled=True)  47.9 us
    pallas_call x1, Pallas kernels, on_device(): pl.pallas_call(post_kernel, out_shape=jax.ShapeDtypeStruct((byte_rows, oc...  12.4 us
    broadcast_in_dim x4, local copies, waits for them, and re-layouts, widening_blocks(): blocks = jnp.where(eye, wf, jnp.zeros((), wf.dtype))  10.7 us
    pallas_call x1, Pallas kernels, on_device(): pl.pallas_call(functools.partial(shorten_kernel, parts='kv'), out_shape=j...  6.77 us
    pallas_call x1, Pallas kernels, on_device(): pl.pallas_call(functools.partial(shorten_kernel, parts='q'), out_shape=ja...  5.56 us
  transfers between devices with their start and end apart: 2, of which 2 were waited for; matrix products, arithmetic and copies ran while one was open for 14% of the time, Pallas kernels for 5%

profile of v9, /device:TPU:6, one launch (start us, length us, event | category | flops | bytes accessed | tf_op | source)
XLA Modules:
  0.0 104.2 jit_solution(17134585123704954276)
XLA Ops:
  6.5 0.0 all-gather.2.cloned.1.call-start
  6.5 0.8 slice.3
  7.3 1.7 %collective-permute-start = (bf16[3,2048]{1,0:T(4,128)(2,1)S(1)}, bf16[3,2048]{1,0:T(4,128)(2,1)S(1)}, u32[]{:S(2)}, u32[]{:S(2)}) collective-permute-start(bf16[3,2048]{1,0:T(4,128)(2,1)S(1)} %slice.3), channel_id=1, source_target_pairs={{0,1},{1,2},{2,3},{3,4},{4,5},{5,6},{6,7},{7,8},{8,9},{9,10},{10,1... | collective-permute-start | bytes 36872 | tf_op jit(solution)/shard_map/ppermute | solution.py:16
  9.1 0.8 collective-permute-done.rim_ref
  9.9 0.0 copy-start.2
  9.9 0.6 copy-done.2
  10.5 0.0 copy-start.1
  10.5 6.8 %shard_map.56 = bf16[2,1,8,128,128]{4,3,2,1,0:T(8,128)(2,1)} custom-call(bf16[512,2048]{1,0:T(8,128)(2,1)} %res_ref.5, bf16[3,2048]{1,0:T(4,128)(2,1)} %copy-done.2, bf16[32,96,256]{2,1,0:T(8,128)(2,1)} %bitcast.10), custom_call_target="tpu_custom_call" | custom-call | tf_op jit(solution)/shard_map/pallas_call | solution.py:155
  17.3 0.0 all-gather.2.cloned.1.call-update
  17.3 0.0 copy-done.1
  17.3 0.4 reshape.14
  17.7 0.3 copy.6
  18.0 4.4 %broadcast_in_dim.31 = bf16[4,8,4,32,4,64]{5,4,3,2,0,1:T(4,128)(2,1)} broadcast(bf16[4,8,4,32,64]{4,3,2,0,1:T(8,128)(2,1)S(1)} %copy.6), dimensions={0,1,2,3,5} | broadcast | bytes 2621440 | tf_op jit(solution)/shard_map/jit(_where)/broadcast_in_dim | solution.py:30
  22.4 0.0 copy-start
  22.4 6.0 %broadcast_in_dim.32 = bf16[4,8,128,256]{3,2,0,1:T(8,128)(2,1)S(1)} reshape(bf16[4,8,4,32,4,64]{5,4,3,2,0,1:T(4,128)(2,1)} %broadcast_in_dim.31) | data formatting | bytes 4194304 | tf_op jit(solution)/shard_map/jit(_where)/broadcast_in_dim | solution.py:30
  28.4 0.1 broadcast_in_dim.28
  28.6 0.2 broadcast_in_dim.29
  28.7 0.0 copy-done
  28.7 1.3 %copy.7 = bf16[256,2048]{0,1:T(8,128)(2,1)} copy(bf16[256,2048]{1,0:T(8,128)(2,1)S(1)} %copy-done) | data formatting | bytes 2097152 | tf_op args[1]
  30.0 1.5 %broadcast_select_fusion = bf16[4,8,128,256]{3,2,0,1:T(8,128)(2,1)} fusion(bf16[4,8,128,256]{3,2,0,1:T(8,128)(2,1)S(1)} %broadcast_in_dim.32, pred[128,256]{1,0:T(8,128)(4,1)S(1)} %broadcast_in_dim.29), kind=kLoop, calls=%fused_computation | loop fusion | flops 1048576 | bytes 4227072 | tf_op jit(solution)/shard_map/jit(_where)/select_n | solution.py:30
  31.5 5.6 %shard_map.55.q_ref = bf16[8,128,128]{2,1,0:T(8,128)(2,1)} custom-call(bf16[512,2048]{1,0:T(8,128)(2,1)} %res_ref.5, bf16[3,2048]{1,0:T(4,128)(2,1)} %copy-done.2, bf16[32,96,256]{2,1,0:T(8,128)(2,1)} %bitcast.11), custom_call_target="tpu_custom_call" | custom-call | tf_op jit(solution)/shard_map/pallas_call | solution.py:163
  37.1 47.9 %all-gather.2.cloned.1.call-done.kv_ref = bf16[2,16,8,128,128]{4,3,2,1,0:T(8,128)(2,1)} async-done(((bf16[2,1,8,128,128]{4,3,2,1,0:T(8,128)(2,1)}), bf16[2,16,8,128,128]{4,3,2,1,0:T(8,128)(2,1)}) %all-gather.2.cloned.1.call-update) | async-done | bytes 8388624 | tf_op jit(solution)/shard_map/all_gather | solution.py:162
  85.0 12.4 %shard_map.57 = bf16[512,256]{1,0:T(8,128)(2,1)} custom-call(s32[1]{0:T(128)} %bitcast.idx_ref, f32[8]{0:T(128)} %sharp_ref.1, bf16[8,128,128]{2,1,0:T(8,128)(2,1)} %shard_map.55.q_ref, bf16[2,16,8,128,128]{4,3,2,1,0:T(8,128)(2,1)} %all-gather.2.cloned.1.call-done.kv_ref, bf16[8,512,256]{2,1,0:T(8,128)(2,1)} %bitcast.9, bf16[512,2048]{1,0:T(8,128)(2,1)} %res_ref.5, ...), custom_call_target="tpu_custom_call" | custom-call | tf_op jit(solution)/shard_map/pallas_call | solution.py:172
  (1 shorter events, 0.0 us)
Async XLA Ops:
  6.5 78.4 %all-gather.2.cloned.1.call-start = ((), (), s32[]{:S(2)}) async-start(), calls=%async_computation | async-start | bytes 8912896 | tf_op jit(solution)/shard_map/all_gather | solution.py:162
  7.3 2.6 %collective-permute-start = (bf16[3,2048]{1,0:T(4,128)(2,1)S(1)}, bf16[3,2048]{1,0:T(4,128)(2,1)S(1)}, u32[]{:S(2)}, u32[]{:S(2)}) collective-permute-start(bf16[3,2048]{1,0:T(4,128)(2,1)S(1)} %slice.3), channel_id=1, source_target_pairs={{0,1},{1,2},{2,3},{3,4},{4,5},{5,6},{6,7},{7,8},{8,9},{9,10},{10,1... | collective-permute-start | bytes 36872 | tf_op jit(solution)/shard_map/ppermute | solution.py:16
  9.9 0.6 copy-start.2
  10.5 6.8 %copy-start.1 = (bf16[32,32,256]{2,1,0:T(8,128)(2,1)S(1)}, bf16[32,32,256]{2,1,0:T(8,128)(2,1)}, u32[]{:S(2)}) copy-start(bf16[32,32,256]{2,1,0:T(8,128)(2,1)} %param.9) | copy-start | bytes 1572868
  22.4 6.3 %copy-start = (bf16[256,2048]{1,0:T(8,128)(2,1)S(1)}, bf16[256,2048]{1,0:T(8,128)(2,1)}, u32[]{:S(2)}) copy-start(bf16[256,2048]{1,0:T(8,128)(2,1)} %param.6) | copy-start | bytes 3145732
Sparse Core Ops, SparseCore 0:
  17.4 67.5 all-gather.1

commit v10 on v9

--- a/solution.py
+++ b/solution.py
@@ -96,11 +96,13 @@
         q = q_ref[h]
         sharp = sharp_ref[h]
         keys_t = jnp.concatenate([kv_ref[0, d, h] for d in range(nb)], axis=1)
-        vals = jnp.concatenate([kv_ref[1, d, h] for d in range(nb)], axis=0)
         s = jnp.dot(q, keys_t, preferred_element_type=f32) * sharp
         w = jnp.where(visible, jnp.exp(s - sharp), jnp.zeros((), f32))
         den = jnp.sum(w, axis=1, keepdims=True)
-        num = jnp.dot(w.astype(bf16), vals, preferred_element_type=f32)
+        w_low = w.astype(bf16)
+        num = jnp.dot(w_low[:, :tq], kv_ref[1, 0, h], preferred_element_type=f32)
+        for d in range(1, nb):
+            num = num + jnp.dot(w_low[:, d * tq : (d + 1) * tq], kv_ref[1, d, h], preferred_element_type=f32)
         att_scr[:, h * hd : (h + 1) * hd] = (num / den).astype(bf16)
 
     rows, width = res_ref.shape

time: 106 us -> 105 us (level)
  no operation moved by 1% of the time
where the time goes in v10:
time: 105 us; the launch traced here: 104 us
  waiting for transfers between devices  48.7 us (46%)
  Pallas kernels  24.4 us (23%)
  local copies, waits for them, and re-layouts  14.1 us (13%)
  between operations  13.5 us (13%)
  starting transfers between devices  1.74 us (2%)
  other arithmetic  1.5 us (1%)
    all_gather x1, waiting for transfers between devices, on_device(): gathered = lax.all_gather(stacked, 'seq', axis=1, tiled=True)  47.9 us
    pallas_call x1, Pallas kernels, on_device(): pl.pallas_call(post_kernel, out_shape=jax.ShapeDtypeStruct((byte_rows, oc...  12.1 us
    broadcast_in_dim x4, local copies, waits for them, and re-layouts, widening_blocks(): blocks = jnp.where(eye, wf, jnp.zeros((), wf.dtype))  10.7 us
    pallas_call x1, Pallas kernels, on_device(): pl.pallas_call(functools.partial(shorten_kernel, parts='kv'), out_shape=j...  6.77 us
    pallas_call x1, Pallas kernels, on_device(): pl.pallas_call(functools.partial(shorten_kernel, parts='q'), out_shape=ja...  5.56 us
  transfers between devices with their start and end apart: 2, of which 2 were waited for; matrix products, arithmetic and copies ran while one was open for 14% of the time, Pallas kernels for 5%

profile of v10, /device:TPU:6, one launch (start us, length us, event | category | flops | bytes accessed | tf_op | source)
XLA Modules:
  0.0 103.9 jit_solution(8532256933709962088)
XLA Ops:
  6.5 0.0 all-gather.2.cloned.1.call-start
  6.5 0.8 slice.3
  7.3 1.7 %collective-permute-start = (bf16[3,2048]{1,0:T(4,128)(2,1)S(1)}, bf16[3,2048]{1,0:T(4,128)(2,1)S(1)}, u32[]{:S(2)}, u32[]{:S(2)}) collective-permute-start(bf16[3,2048]{1,0:T(4,128)(2,1)S(1)} %slice.3), channel_id=1, source_target_pairs={{0,1},{1,2},{2,3},{3,4},{4,5},{5,6},{6,7},{7,8},{8,9},{9,10},{10,1... | collective-permute-start | bytes 36872 | tf_op jit(solution)/shard_map/ppermute | solution.py:16
  9.1 0.8 collective-permute-done.rim_ref
  9.9 0.0 copy-start.2
  9.9 0.6 copy-done.2
  10.5 0.0 copy-start.1
  10.5 6.8 %shard_map.56 = bf16[2,1,8,128,128]{4,3,2,1,0:T(8,128)(2,1)} custom-call(bf16[512,2048]{1,0:T(8,128)(2,1)} %res_ref.5, bf16[3,2048]{1,0:T(4,128)(2,1)} %copy-done.2, bf16[32,96,256]{2,1,0:T(8,128)(2,1)} %bitcast.10), custom_call_target="tpu_custom_call" | custom-call | tf_op jit(solution)/shard_map/pallas_call | solution.py:157
  17.3 0.0 all-gather.2.cloned.1.call-update
  17.3 0.0 copy-done.1
  17.3 0.4 reshape.14
  17.7 0.3 copy.6
  18.0 4.4 %broadcast_in_dim.31 = bf16[4,8,4,32,4,64]{5,4,3,2,0,1:T(4,128)(2,1)} broadcast(bf16[4,8,4,32,64]{4,3,2,0,1:T(8,128)(2,1)S(1)} %copy.6), dimensions={0,1,2,3,5} | broadcast | bytes 2621440 | tf_op jit(solution)/shard_map/jit(_where)/broadcast_in_dim | solution.py:30
  22.4 0.0 copy-start
  22.4 6.0 %broadcast_in_dim.32 = bf16[4,8,128,256]{3,2,0,1:T(8,128)(2,1)S(1)} reshape(bf16[4,8,4,32,4,64]{5,4,3,2,0,1:T(4,128)(2,1)} %broadcast_in_dim.31) | data formatting | bytes 4194304 | tf_op jit(solution)/shard_map/jit(_where)/broadcast_in_dim | solution.py:30
  28.4 0.1 broadcast_in_dim.28
  28.6 0.2 broadcast_in_dim.29
  28.7 0.0 copy-done
  28.7 1.3 %copy.7 = bf16[256,2048]{0,1:T(8,128)(2,1)} copy(bf16[256,2048]{1,0:T(8,128)(2,1)S(1)} %copy-done) | data formatting | bytes 2097152 | tf_op args[1]
  30.0 1.5 %broadcast_select_fusion = bf16[4,8,128,256]{3,2,0,1:T(8,128)(2,1)} fusion(bf16[4,8,128,256]{3,2,0,1:T(8,128)(2,1)S(1)} %broadcast_in_dim.32, pred[128,256]{1,0:T(8,128)(4,1)S(1)} %broadcast_in_dim.29), kind=kLoop, calls=%fused_computation | loop fusion | flops 1048576 | bytes 4227072 | tf_op jit(solution)/shard_map/jit(_where)/select_n | solution.py:30
  31.5 5.6 %shard_map.55.q_ref = bf16[8,128,128]{2,1,0:T(8,128)(2,1)} custom-call(bf16[512,2048]{1,0:T(8,128)(2,1)} %res_ref.5, bf16[3,2048]{1,0:T(4,128)(2,1)} %copy-done.2, bf16[32,96,256]{2,1,0:T(8,128)(2,1)} %bitcast.11), custom_call_target="tpu_custom_call" | custom-call | tf_op jit(solution)/shard_map/pallas_call | solution.py:165
  37.1 47.9 %all-gather.2.cloned.1.call-done.kv_ref = bf16[2,16,8,128,128]{4,3,2,1,0:T(8,128)(2,1)} async-done(((bf16[2,1,8,128,128]{4,3,2,1,0:T(8,128)(2,1)}), bf16[2,16,8,128,128]{4,3,2,1,0:T(8,128)(2,1)}) %all-gather.2.cloned.1.call-update) | async-done | bytes 8388624 | tf_op jit(solution)/shard_map/all_gather | solution.py:164
  85.0 12.1 %shard_map.57 = bf16[512,256]{1,0:T(8,128)(2,1)} custom-call(s32[1]{0:T(128)} %bitcast.idx_ref, f32[8]{0:T(128)} %sharp_ref.1, bf16[8,128,128]{2,1,0:T(8,128)(2,1)} %shard_map.55.q_ref, bf16[2,16,8,128,128]{4,3,2,1,0:T(8,128)(2,1)} %all-gather.2.cloned.1.call-done.kv_ref, bf16[8,512,256]{2,1,0:T(8,128)(2,1)} %bitcast.9, bf16[512,2048]{1,0:T(8,128)(2,1)} %res_ref.5, ...), custom_call_target="tpu_custom_call" | custom-call | tf_op jit(solution)/shard_map/pallas_call | solution.py:174
  (1 shorter events, 0.0 us)
Async XLA Ops:
  6.5 78.4 %all-gather.2.cloned.1.call-start = ((), (), s32[]{:S(2)}) async-start(), calls=%async_computation | async-start | bytes 8912896 | tf_op jit(solution)/shard_map/all_gather | solution.py:164
  7.3 2.6 %collective-permute-start = (bf16[3,2048]{1,0:T(4,128)(2,1)S(1)}, bf16[3,2048]{1,0:T(4,128)(2,1)S(1)}, u32[]{:S(2)}, u32[]{:S(2)}) collective-permute-start(bf16[3,2048]{1,0:T(4,128)(2,1)S(1)} %slice.3), channel_id=1, source_target_pairs={{0,1},{1,2},{2,3},{3,4},{4,5},{5,6},{6,7},{7,8},{8,9},{9,10},{10,1... | collective-permute-start | bytes 36872 | tf_op jit(solution)/shard_map/ppermute | solution.py:16
  9.9 0.6 copy-start.2
  10.5 6.8 %copy-start.1 = (bf16[32,32,256]{2,1,0:T(8,128)(2,1)S(1)}, bf16[32,32,256]{2,1,0:T(8,128)(2,1)}, u32[]{:S(2)}) copy-start(bf16[32,32,256]{2,1,0:T(8,128)(2,1)} %param.9) | copy-start | bytes 1572868
  22.4 6.3 %copy-start = (bf16[256,2048]{1,0:T(8,128)(2,1)S(1)}, bf16[256,2048]{1,0:T(8,128)(2,1)}, u32[]{:S(2)}) copy-start(bf16[256,2048]{1,0:T(8,128)(2,1)} %param.6) | copy-start | bytes 3145732
Sparse Core Ops, SparseCore 0:
  17.4 67.5 all-gather.1
